TPU v7x, 32 devices: a whole 2x2x4 slice. The times are simulated.
32 devices in a mesh: groups: 2 (over x), hits: 8 (over z, y), heads: 2 (over core).
Axes of the slice: x: 2, y: 2, z: 4, core: 2. Of those that a mesh axis runs over, the one named last changes fastest.
Arguments:
- queries: bfloat16 [2048, 2048], P('groups', 'heads'), parts along dimension 0, may hold values from -13.5 to 13.5
- keys: bfloat16 [8192, 2048], P(('groups', 'hits'), 'heads'), parts along dimension 0, may hold values from -36 to 36
- values: bfloat16 [8192, 2048], P(('groups', 'hits'), 'heads'), parts along dimension 0, may hold values from -6 to 6
- hit_counts: int32 [16], P(('groups', 'hits')), parts along dimension 0, may hold values from 128 to 512, as said below
- latents: bfloat16 [2048, 2048], P(('groups', 'hits'), 'heads'), parts along dimension 0, may hold values from -23 to 23
- out_proj: bfloat16 [2048, 2048], P('heads'), may hold values from -1 to 1
- norm_gain: float32 [2048], P('heads'), may hold values from 0.1 to 1.9
- up_proj: bfloat16 [2048, 8192], P('heads', 'hits'), may hold values from -0.125 to 0.125
- down_proj: bfloat16 [8192, 2048], P('hits', 'heads'), may hold values from -0.25 to 0.25
Outputs:
- mixed: bfloat16 [2048, 2048], P(('groups', 'hits'), 'heads'), parts along dimension 0
There are 2 independent parts, one for each index of `groups`. A program takes and returns all parts, laid end to end along the dimension named above; an argument that names none is the same for every part. Nothing has to cross between parts.
Inputs may be any that keep to these rules, and one draw needn't show every extreme that they name: hit_counts[s] live hits fill the first slots of shard s; some shard is full and some holds exactly 128.
All inputs are finite; a program needn't handle non-finite values.
Results may differ from a plain program's by a relative error of at most 0.012.
Values may be sent and summed in bfloat16 or wider, within the bound.
No kernel may reach another device: no remote copies, remote signals or barrier semaphores. Data moves between devices by JAX's collectives and lax.ppermute only.
A program may use at most 64 MiB of HBM per device.

v0:
```python
import math

import jax
import jax.numpy as jnp
from jax import lax
from jax.sharding import PartitionSpec as P

D = 2048
HD = 128


def shards(queries, keys, values, hit_counts, latents, out_proj, norm_gain, up_proj, down_proj):
    width = keys.shape[1]
    local_heads = width // HD
    score_scale = 1.0 / math.sqrt(HD)
    live_mask = lax.broadcasted_iota(jnp.int32, (1, keys.shape[0]), 1) < hit_counts[0]

    def merged(row_top, row_total, context):
        row_best = lax.pmax(row_top, "hits")
        factor = jnp.exp(row_top - row_best)
        total_sum, context_sum = (
            lax.psum_scatter(row_total * factor, "hits", scatter_dimension=1, tiled=True),
            lax.psum_scatter(context * factor[..., None], "hits", scatter_dimension=1, tiled=True),
        )
        return (context_sum / total_sum[..., None]).astype(jnp.bfloat16)

    def one_head(head_index):
        col_start = head_index * HD
        q_head = lax.dynamic_slice_in_dim(queries, col_start, HD, 1)
        k_head = lax.dynamic_slice_in_dim(keys, col_start, HD, 1)
        v_head = lax.dynamic_slice_in_dim(values, col_start, HD, 1)
        scores = (
            lax.dot_general(
                q_head, k_head, (((1,), (1,)), ((), ())), preferred_element_type=jnp.float32
            )
            * score_scale
        )
        scores = jnp.where(live_mask, scores, -1e30)
        row_top = jnp.max(scores, axis=1)
        weights = jnp.where(live_mask, jnp.exp(scores - row_top[:, None]), 0.0)
        row_total = jnp.sum(weights, axis=1)
        context = jnp.dot(weights.astype(jnp.bfloat16), v_head, preferred_element_type=jnp.float32)
        return (row_top, row_total, context)

    context = merged(*lax.map(one_head, jnp.arange(local_heads, dtype=jnp.int32)))
    weights_out = out_proj.reshape(local_heads, HD, out_proj.shape[1])
    projected = jnp.einsum("hrd,hde->re", context, weights_out, preferred_element_type=jnp.float32)
    attended = lax.psum_scatter(projected, "heads", scatter_dimension=1, tiled=True)
    stream = latents.astype(jnp.float32) + attended
    squares = lax.psum(jnp.sum(stream * stream, axis=1), "heads")
    normed = (stream * lax.rsqrt(squares / D + 1e-06)[:, None] * norm_gain[None, :]).astype(
        jnp.bfloat16
    )
    partial_units = jnp.dot(
        lax.all_gather(normed, "hits", axis=0, tiled=True),
        up_proj,
        preferred_element_type=jnp.float32,
    )
    summed_units = lax.psum(partial_units, "heads")
    hidden = jax.nn.gelu(summed_units).astype(jnp.bfloat16)
    branch_out = lax.psum_scatter(
        jnp.dot(hidden, down_proj, preferred_element_type=jnp.float32),
        "hits",
        scatter_dimension=0,
        tiled=True,
    )
    return (stream + branch_out).astype(jnp.bfloat16)


def solution(mesh):
    return jax.shard_map(
        shards,
        mesh=mesh,
        in_specs=(
            P("groups", "heads"),
            P(("groups", "hits"), "heads"),
            P(("groups", "hits"), "heads"),
            P(("groups", "hits")),
            P(("groups", "hits"), "heads"),
            P("heads", None),
            P("heads"),
            P("heads", "hits"),
            P("hits", "heads"),
        ),
        out_specs=P(("groups", "hits"), "heads"),
        check_vma=False,
    )
```

profile of v0, /device:TPU:0, one launch (start us, length us, event | category | flops | bytes accessed | tf_op | source)
XLA Modules:
  0.0 451.4 jit_solution(14915383482989247984)
XLA Ops:
  6.5 54.9 %while.15 = (s32[]{:T(128)}, f32[8,1024]{1,0:T(8,128)S(1)}, f32[8,1024]{1,0:T(8,128)S(1)}, f32[8,1024,128]{2,1,0:T(8,128)}, s32[8]{0:T(128)S(1)}, /*index=5*/bf1...) while((s32[]{:T(128)}, f32[8,1024]{1,0:T(8,128)S(1)}, ...), condition=%wide.region_3.4_spmd.clone, body=%wide.region_0.3_spmd.clone.sunk | while | flops 275249664 | bytes 7376583 | solution.py:45
  6.6 0.7 dynamic_slice.34
  7.9 0.7 compare_reduce_fusion.2
  8.6 1.4 fusion.52
  10.1 2.5 fusion.54
  13.4 0.7 dynamic_slice.34
  14.8 0.7 compare_reduce_fusion.2
  15.4 1.4 fusion.52
  16.9 2.6 fusion.54
  20.3 0.7 dynamic_slice.34
  21.6 0.7 compare_reduce_fusion.2
  22.3 1.4 fusion.52
  23.8 2.6 fusion.54
  27.1 0.7 dynamic_slice.34
  28.5 0.7 compare_reduce_fusion.2
  29.2 1.4 fusion.52
  30.6 2.6 fusion.54
  34.0 0.7 dynamic_slice.34
  35.4 0.7 compare_reduce_fusion.2
  36.0 1.4 fusion.52
  37.5 2.6 fusion.54
  40.9 0.7 dynamic_slice.34
  42.2 0.7 compare_reduce_fusion.2
  42.9 1.4 fusion.52
  44.4 2.6 fusion.54
  47.7 0.7 dynamic_slice.34
  49.1 0.7 compare_reduce_fusion.2
  49.8 1.5 fusion.52
  51.2 2.5 fusion.54
  54.6 0.7 dynamic_slice.34
  56.0 0.7 compare_reduce_fusion.2
  56.6 1.4 fusion.52
  58.1 2.6 fusion.54
  61.5 38.9 %pmax.7 = f32[8,1024]{1,0:T(8,128)S(1)} all-reduce(f32[8,1024]{1,0:T(8,128)S(1)} %get-tuple-element.55), channel_id=1, replica_groups=mesh['groups'=2,'hits'=8,'heads'=2] {'hits'}, use_global_device_ids=true, to_apply=%region_4.5 | all-reduce | flops 8192 | bytes 65536 | tf_op jit(solution)/shard_map/pmax | solution.py:19
  101.0 4.2 broadcast_multiply_fusion
  105.3 47.9 %reduce-scatter.7.cloned.1.call-done = f32[8,128]{1,0:T(8,128)} async-done(((f32[8,1024]{1,0:T(8,128)}), f32[8,128]{1,0:T(8,128)}) %reduce-scatter.7.cloned.1.call-update) | async-done | bytes 4112 | tf_op jit(solution)/shard_map/reduce_scatter | solution.py:22
  153.2 91.0 %reduce-scatter.5.cloned.1.call-done = f32[8,128,128]{2,1,0:T(8,128)} async-done(((f32[8,1024,128]{2,1,0:T(8,128)}), f32[8,128,128]{2,1,0:T(8,128)}) %reduce-scatter.5.cloned.1.call-update) | async-done | bytes 524304 | tf_op jit(solution)/shard_map/reduce_scatter | solution.py:23
  244.2 4.2 convolution_bitcast_fusion.1
  248.4 8.1 %reduce-scatter.9.cloned.1.call-done = f32[128,1024]{1,0:T(8,128)} async-done(((f32[128,2048]{1,0:T(8,128)}), f32[128,1024]{1,0:T(8,128)}) %reduce-scatter.9.cloned.1.call-update) | async-done | bytes 524304 | tf_op jit(solution)/shard_map/reduce_scatter | solution.py:48
  256.5 1.2 multiply_reduce_fusion
  257.7 2.5 psum.14
  260.2 1.9 multiply_convert_fusion
  262.1 50.4 %all-gather.2.cloned.1.call-done = bf16[1024,1024]{1,0:T(8,128)(2,1)} async-done(((bf16[128,1024]{1,0:T(8,128)(2,1)}), bf16[1024,1024]{1,0:T(8,128)(2,1)}) %all-gather.2.cloned.1.call-update) | async-done | bytes 2097168 | tf_op jit(solution)/shard_map/all_gather | solution.py:55
  312.5 5.9 %fusion.40 = f32[1024,1024]{1,0:T(8,128)} fusion(bf16[1024,1024]{1,0:T(8,128)(2,1)} %all-gather.2.cloned.1.call-done, bf16[1024,1024]{1,0:T(8,128)(2,1)S(1)} %copy-done), kind=kOutput, calls=%fused_computation.51 | convolution fusion | flops 2147483648 | bytes 8388608 | tf_op jit(solution)/shard_map/dot_general | solution.py:54
  318.5 26.7 %all-reduce.2.cloned.1.call-done = f32[1024,1024]{1,0:T(8,128)} async-done(((f32[1024,1024]{1,0:T(8,128)}), f32[1024,1024]{1,0:T(8,128)}) %all-reduce.2.cloned.1.call-update) | async-done | bytes 4194320 | tf_op jit(solution)/shard_map/psum | solution.py:59
  345.2 7.5 %fusion.28 = f32[1024,1024]{1,0:T(8,128)} fusion(bf16[1024,1024]{1,0:T(8,128)(2,1)} %param.19, f32[1024,1024]{1,0:T(8,128)} %all-reduce.2.cloned.1.call-done), kind=kOutput, calls=%fused_computation.32 | convolution fusion | flops 2156920832 | bytes 10485760 | tf_op jit(solution)/shard_map/dot_general | solution.py:62
  352.7 90.0 %reduce-scatter.11.cloned.1.call-done = f32[128,1024]{1,0:T(8,128)} async-done(((f32[1024,1024]{1,0:T(8,128)}), f32[128,1024]{1,0:T(8,128)}) %reduce-scatter.11.cloned.1.call-update) | async-done | bytes 524304 | tf_op jit(solution)/shard_map/reduce_scatter | solution.py:61
  442.8 1.8 add_convert_fusion
  (50 shorter events, 7.2 us)
Async XLA Ops:
  6.5 306.0 %copy-start = (bf16[1024,1024]{1,0:T(8,128)(2,1)S(1)}, bf16[1024,1024]{1,0:T(8,128)(2,1)}, u32[]{:S(2)}) copy-start(bf16[1024,1024]{1,0:T(8,128)(2,1)} %param.18) | copy-start | bytes 6291460
  6.5 146.6 %reduce-scatter.7.cloned.1.call-start = ((), (), s32[]{:S(2)}) async-start(), calls=%async_computation.5 | async-start | bytes 36864 | tf_op jit(solution)/shard_map/reduce_scatter | solution.py:22
  101.0 143.2 %reduce-scatter.5.cloned.1.call-start = ((), (), s32[]{:S(2)}) async-start(), calls=%async_computation.4 | async-start | bytes 4718592 | tf_op jit(solution)/shard_map/reduce_scatter | solution.py:23
  105.3 151.3 %reduce-scatter.9.cloned.1.call-start = ((), (), s32[]{:S(2)}) async-start(), calls=%async_computation.6 | async-start | bytes 1572864 | tf_op jit(solution)/shard_map/reduce_scatter | solution.py:48
  244.2 12.4 %copy-start.2 = (bf16[128,1024]{1,0:T(8,128)(2,1)S(1)}, bf16[128,1024]{1,0:T(8,128)(2,1)}, u32[]{:S(2)}) copy-start(bf16[128,1024]{1,0:T(8,128)(2,1)} %param.15) | copy-start | bytes 786436
  244.2 16.0 %copy-start.3 = (f32[1024]{0:T(1024)S(1)}, f32[1024]{0:T(1024)}, u32[]{:S(2)}) copy-start(f32[1024]{0:T(1024)} %param.17) | copy-start | bytes 12292
  248.4 64.2 %all-gather.2.cloned.1.call-start = ((), (), s32[]{:S(2)}) async-start(), calls=%async_computation.7 | async-start | bytes 2359296 | tf_op jit(solution)/shard_map/all_gather | solution.py:55
  262.1 83.1 %all-reduce.2.cloned.1.call-start = ((), (), s32[]{:S(2)}) async-start(), calls=%async_computation.8 | async-start | bytes 8388608 | tf_op jit(solution)/shard_map/psum | solution.py:59
  318.5 124.3 %reduce-scatter.11.cloned.1.call-start = ((), (), s32[]{:S(2)}) async-start(), calls=%async_computation.9 | async-start | bytes 4718592 | tf_op jit(solution)/shard_map/reduce_scatter | solution.py:61
  352.7 90.1 %copy-start.1 = (f32[128,1024]{1,0:T(8,128)S(1)}, f32[128,1024]{1,0:T(8,128)}, u32[]{:S(2)}) copy-start(f32[128,1024]{1,0:T(8,128)} %reduce-scatter.9.cloned.1.call-done) | copy-start | bytes 1572868
Sparse Core Ops, SparseCore 0:
  101.1 52.0 reduce-scatter.6
  156.8 87.3 reduce-scatter.4
  248.5 8.0 reduce-scatter.8
  262.2 50.2 all-gather.1
  318.6 26.6 all-reduce.1
  352.9 89.8 reduce-scatter.10
where the time goes:
time: 452 us; the launch traced here: 451 us
  waiting for transfers between devices  314 us (69%)
  matrix products  49.5 us (11%)
  blocking collectives  41.3 us (9%)
  other arithmetic  19.6 us (4%)
  between operations  13.5 us (3%)
  local copies, waits for them, and re-layouts  7.08 us (2%)
  loops' own time  5.98 us (1%)
    reduce_scatter x1, waiting for transfers between devices, merged(): lax.psum_scatter(context * factor[..., None], 'hits', scatter_dimension=1...  91 us
    reduce_scatter x1, waiting for transfers between devices, shards(): lax.psum_scatter(jnp.dot(hidden, down_proj, preferred_element_type=jnp.fl...  90 us
    all_gather x1, waiting for transfers between devices, shards(): lax.all_gather(normed, 'hits', axis=0, tiled=True)  50.4 us
    reduce_scatter x1, waiting for transfers between devices, merged(): lax.psum_scatter(row_total * factor, 'hits', scatter_dimension=1, tiled=T...  47.9 us
    pmax x1, blocking collectives, merged(): row_best = lax.pmax(row_top, 'hits')  38.9 us
    psum x1, waiting for transfers between devices, shards(): summed_units = lax.psum(partial_units, 'heads')  26.7 us
    dot_general x8, matrix products, one_head(): jnp.dot(weights.astype(jnp.bfloat16), v_head, preferred_element_type=jnp....  20.5 us
    dot_general x8, matrix products, one_head(): lax.dot_general(q_head, k_head, (((1,), (1,)), ((), ())), preferred_eleme...  11.6 us
  transfers between devices with their start and end apart: 6, of which 6 were waited for; matrix products, arithmetic and copies ran while one was open for 1% of the time, Pallas kernels for 0%

commit v1 on v0

v1 whole, which is shorter than its diff:
```python
import functools
import math

import jax
import jax.numpy as jnp
from jax import lax
from jax.experimental import pallas as pl
from jax.experimental.pallas import tpu as pltpu
from jax.sharding import PartitionSpec as P

HD = 128
BF = jnp.bfloat16
F32 = jnp.float32
EXP_SCALE = math.log2(math.e) / math.sqrt(HD)
DEAD = -1e30


def attn_kernel(heads, blocks, idx_ref, cnt_ref, *refs):
    q_refs, (k_ref, v_ref, ctx_ref, st_ref) = refs[:blocks], refs[blocks:]
    hits = k_ref.shape[0]
    live = lax.broadcasted_iota(jnp.int32, (hits, 1), 0) < cnt_ref[0]
    tops, sums = [], []
    for h in range(heads):
        cols = slice(h * HD, (h + 1) * HD)
        qh = q_refs[0][:, cols]
        if blocks > 1:
            qh = jnp.concatenate([r[:, cols] for r in q_refs], axis=0)
        s = lax.dot_general(k_ref[:, cols], qh, (((1,), (1,)), ((), ())), preferred_element_type=F32)
        s = jnp.where(live, s, DEAD)
        top = jnp.max(s, axis=0, keepdims=True).astype(BF).astype(F32)
        p = jnp.exp2((s - top) * EXP_SCALE)
        tops.append(top)
        sums.append(jnp.sum(p, axis=0, keepdims=True))
        ctx_ref[cols, :] = lax.dot_general(
            v_ref[:, cols], p.astype(BF), (((0,), (0,)), ((), ())), preferred_element_type=F32
        )
    st_ref[...] = jnp.concatenate(tops + sums, axis=0)


def attend(idx, cnt, q, k, v, rows):
    blocks = idx.shape[0]
    width, hits = k.shape[1], k.shape[0]
    heads = width // HD
    n = blocks * rows

    def q_spec(b):
        return pl.BlockSpec((rows, width), lambda i, idx_r, cnt_r: (idx_r[b], 0))

    whole = lambda shape: pl.BlockSpec(shape, lambda i, idx_r, cnt_r: (0, 0))
    return pl.pallas_call(
        functools.partial(attn_kernel, heads, blocks),
        grid_spec=pltpu.PrefetchScalarGridSpec(
            num_scalar_prefetch=2,
            grid=(1,),
            in_specs=[q_spec(b) for b in range(blocks)] + [whole(k.shape), whole(v.shape)],
            out_specs=[whole((width, n)), whole((2 * heads, n))],
        ),
        out_shape=[
            jax.ShapeDtypeStruct((width, n), F32),
            jax.ShapeDtypeStruct((2 * heads, n), F32),
        ],
        cost_estimate=pl.CostEstimate(
            flops=4 * n * hits * width,
            bytes_accessed=2 * k.size * 2 + n * width * 6,
            transcendentals=n * hits * heads,
        ),
        name="attend",
    )(idx, cnt, *([q] * blocks), k, v)


def group_rows(gh):
    return gh * HD + 4 * gh


def read_group(msg_ref, base, gh):
    st = msg_ref[base + gh * HD : base + gh * HD + 4 * gh, :].astype(F32)
    return st[:gh], st[gh : 2 * gh] + st[2 * gh : 3 * gh]


def write_stats(out_ref, base, gh, top, total):
    hi = total.astype(BF).astype(F32)
    st = jnp.concatenate([top, hi, total - hi, jnp.zeros_like(top)], axis=0)
    out_ref[base + gh * HD : base + gh * HD + 4 * gh, :] = st.astype(BF)


def merge_kernel(heads, jobs, lo, rows, *refs):
    gh = heads // 2
    gr = group_rows(gh)
    ctx_ref, st_ref = refs[0], refs[1]
    n_msg = sum(1 for j in jobs if j[2])
    msgs, outs = refs[2 : 2 + n_msg], refs[2 + n_msg :]
    at = 0
    for (b, groups, held), out_ref in zip(jobs, outs):
        cols = slice(b * rows, (b + 1) * rows)
        msg_ref = None
        if held:
            msg_ref = msgs[at]
            at += 1
        for g in groups:
            base = groups.index(g) * gr
            top = st_ref[g * gh : (g + 1) * gh, cols]
            total = st_ref[heads + g * gh : heads + (g + 1) * gh, cols]
            if g in held:
                mbase = held.index(g) * gr
                mtop, mtotal = read_group(msg_ref, mbase, gh)
                best = jnp.maximum(top, mtop)
                fa = jnp.exp2((top - best) * EXP_SCALE)
                fb = jnp.exp2((mtop - best) * EXP_SCALE)
                for h in range(gh):
                    src = slice((g * gh + h) * HD, (g * gh + h + 1) * HD)
                    mrc = slice(mbase + h * HD, mbase + (h + 1) * HD)
                    out_ref[base + h * HD : base + (h + 1) * HD, :] = (
                        ctx_ref[src, cols] * fa[h : h + 1]
                        + msg_ref[mrc, :].astype(F32) * fb[h : h + 1]
                    ).astype(BF)
                write_stats(out_ref, base, gh, best, total * fa + mtotal * fb)
            else:
                src = slice(g * gh * HD, (g + 1) * gh * HD)
                out_ref[base : base + gh * HD, :] = ctx_ref[src, cols].astype(BF)
                write_stats(out_ref, base, gh, top, total)


def merge(ctx, st, msgs, jobs, heads, rows):
    gr = group_rows(heads // 2)
    outs = [jax.ShapeDtypeStruct((len(j[1]) * gr, rows), BF) for j in jobs]
    nbytes = sum(len(j[1]) * gr * rows * 8 for j in jobs)
    return pl.pallas_call(
        functools.partial(merge_kernel, heads, jobs, 0, rows),
        out_shape=outs,
        cost_estimate=pl.CostEstimate(flops=nbytes, bytes_accessed=nbytes, transcendentals=0),
        name="merge",
    )(ctx, st, *msgs)


def finish_kernel(heads, rows, ctx_ref, st_ref, a_ref, b_ref, out_ref):
    gh = heads // 2
    gr = group_rows(gh)
    for g in range(2):
        top = st_ref[g * gh : (g + 1) * gh, :]
        total = st_ref[heads + g * gh : heads + (g + 1) * gh, :]
        atop, atotal = read_group(a_ref, g * gr, gh)
        btop, btotal = read_group(b_ref, g * gr, gh)
        best = jnp.maximum(jnp.maximum(top, atop), btop)
        f0 = jnp.exp2((top - best) * EXP_SCALE)
        fa = jnp.exp2((atop - best) * EXP_SCALE)
        fb = jnp.exp2((btop - best) * EXP_SCALE)
        total = total * f0 + atotal * fa + btotal * fb
        f0, fa, fb = f0 / total, fa / total, fb / total
        for h in range(gh):
            src = slice((g * gh + h) * HD, (g * gh + h + 1) * HD)
            mrc = slice(g * gr + h * HD, g * gr + (h + 1) * HD)
            c = (
                ctx_ref[src, :] * f0[h : h + 1]
                + a_ref[mrc, :].astype(F32) * fa[h : h + 1]
                + b_ref[mrc, :].astype(F32) * fb[h : h + 1]
            )
            out_ref[:, src] = jnp.transpose(c).astype(BF)


def finish(ctx, st, a, b, heads, rows):
    return pl.pallas_call(
        functools.partial(finish_kernel, heads, rows),
        out_shape=jax.ShapeDtypeStruct((rows, heads * HD), BF),
        cost_estimate=pl.CostEstimate(
            flops=rows * heads * HD * 8, bytes_accessed=rows * heads * HD * 10, transcendentals=0
        ),
        name="finish",
    )(ctx, st, a, b)


def make_shards(n):
    half = n // 2
    order = list(range(0, n, 2)) + list(range(n - 1, 0, -2))
    fwd = [(order[i], order[(i + 1) % n]) for i in range(n)]
    bwd = [(b, a) for a, b in fwd]
    swap = [(0, 1), (1, 0)]

    right = lambda x: lax.ppermute(x, "hits", fwd)
    left = lambda x: lax.ppermute(x, "hits", bwd)
    partner = lambda x: lax.ppermute(x, "heads", swap)

    def shards(queries, keys, values, hit_counts, latents, out_proj, norm_gain, up_proj, down_proj):
        core = lax.axis_index("heads")
        me = lax.axis_index("hits")
        pos = jnp.where(me % 2 == 0, me // 2, n - 1 - me // 2)

        def block_at(k):
            p = lax.rem(pos + (k + n), n)
            return jnp.where(p < half, 2 * p, 2 * (n - 1 - p) + 1)

        rows = latents.shape[0]
        mine = rows // 2
        width = keys.shape[1]
        heads = width // HD
        feats = 2 * latents.shape[1]
        fh = latents.shape[1]
        cnt = hit_counts.astype(jnp.int32)

        up_oth = partner(up_proj)
        down_oth = partner(down_proj)
        gain_oth = partner(norm_gain.reshape(1, fh))
        gain = jnp.concatenate([norm_gain.reshape(1, fh), gain_oth], axis=1)
        lat_mine = lax.dynamic_slice_in_dim(latents, core * mine, mine, 0)
        lat_oth = partner(lax.dynamic_slice_in_dim(latents, (1 - core) * mine, mine, 0))
        lat = jnp.concatenate([lat_mine, lat_oth], axis=1).astype(F32)

        def partial(ks):
            idx = jnp.stack([block_at(k) for k in ks]).astype(jnp.int32)
            return attend(idx, cnt, queries, keys, values, rows)

        ctx, st = partial([half])
        msg_r, msg_l = merge(ctx, st, [], ((0, (0,), ()), (0, (1,), ())), heads, rows)
        held_r, held_l = (0,), (1,)
        for t in range(2, half + 1):
            msg_r, msg_l = right(msg_r), left(msg_l)
            ctx, st = partial([half - t + 1, t - 1 - half])
            msg_r, msg_l = merge(
                ctx, st, [msg_r, msg_l], ((0, (0, 1), held_r), (1, (0, 1), held_l)), heads, rows
            )
            held_r = held_l = (0, 1)
        msg_r, msg_l = right(msg_r), left(msg_l)
        ctx, st = partial([0])
        context = finish(ctx, st, msg_r, msg_l, heads, rows)

        proj = jnp.dot(context, out_proj, preferred_element_type=F32)

        def own_first(x):
            a, b = x[:, :fh], x[:, fh:]
            return jnp.concatenate([jnp.where(core == 0, a, b), jnp.where(core == 0, b, a)], axis=1)

        proj_mine = lax.dynamic_slice_in_dim(proj, core * mine, mine, 0)
        proj_oth = partner(lax.dynamic_slice_in_dim(proj, (1 - core) * mine, mine, 0))
        stream = lat + own_first(proj_mine + proj_oth)
        squares = jnp.mean(stream * stream, axis=1, keepdims=True)
        normed = (stream * lax.rsqrt(squares + 1e-06) * gain).astype(BF)

        def ffn(x):
            pre = jnp.dot(x[:, :fh], up_proj, preferred_element_type=F32) + jnp.dot(
                x[:, fh:], up_oth, preferred_element_type=F32
            )
            hid = jax.nn.gelu(pre).astype(BF)
            return jnp.concatenate(
                [
                    jnp.dot(hid, down_proj, preferred_element_type=F32),
                    jnp.dot(hid, down_oth, preferred_element_type=F32),
                ],
                axis=1,
            )

        hm = mine // 2
        from_l, from_r = normed, normed
        outs = {}
        own = ffn(normed)
        for s in range(1, half):
            from_l, from_r = right(from_l), left(from_r)
            y = ffn(jnp.concatenate([from_l, from_r], axis=0))
            outs[-s], outs[s] = y[:mine], y[mine:]
        last_l, last_r = right(from_l[:hm]), left(from_r[hm:])
        far = ffn(jnp.concatenate([last_l, last_r], axis=0)).astype(BF)

        msg_r, msg_l = right(far[:hm]), left(far[hm:])
        for t in range(2, half + 1):
            a, b = outs[half - t + 1], outs[t - 1 - half]
            if t == 2:
                a = jnp.concatenate([a[:hm] + msg_r.astype(F32), a[hm:]], axis=0)
                b = jnp.concatenate([b[:hm], b[hm:] + msg_l.astype(F32)], axis=0)
            else:
                a, b = a + msg_r.astype(F32), b + msg_l.astype(F32)
            msg_r, msg_l = right(a.astype(BF)), left(b.astype(BF))
        total = stream + own + msg_r.astype(F32) + msg_l.astype(F32)
        total = total.astype(BF)
        keep, give = total[:, :fh], partner(total[:, fh:])
        return jnp.where(
            core == 0,
            jnp.concatenate([keep, give], axis=0),
            jnp.concatenate([give, keep], axis=0),
        )

    return shards


def solution(mesh):
    return jax.shard_map(
        make_shards(mesh.shape["hits"]),
        mesh=mesh,
        in_specs=(
            P("groups", "heads"),
            P(("groups", "hits"), "heads"),
            P(("groups", "hits"), "heads"),
            P(("groups", "hits")),
            P(("groups", "hits"), "heads"),
            P("heads", None),
            P("heads"),
            P("heads", "hits"),
            P("hits", "heads"),
        ),
        out_specs=P(("groups", "hits"), "heads"),
        check_vma=False,
    )
```

time: 452 us -> 143 us (0.32)
  waiting for transfers between devices: 314 us -> 37.7 us
  blocking collectives: 41.3 us -> 0 us
  Pallas kernels: 0 us -> 39.1 us
  starting transfers between devices: 0.21 us -> 27.1 us
  matrix products: 49.5 us -> 28.5 us
  other arithmetic: 19.6 us -> 4.12 us
  between operations: 13.5 us -> 1.13 us
  loops' own time: 5.98 us -> 0 us
    reduce_scatter x4 -> x0, waiting for transfers between devices: 237 us -> none  [the longest x1 91 us: merged(): lax.psum_scatter(context * factor[..., None], 'hits', scatter_dimension=1...]
    all_gather x1 -> x0, waiting for transfers between devices: 50.4 us -> none  [shards(): lax.all_gather(normed, 'hits', axis=0, tiled=True)]
    pallas_call x0 -> x10, Pallas kernels: none -> 39.1 us  [the longest x5 28.4 us: attend(): pl.pallas_call(functools.partial(attn_kernel, heads, blocks), grid_spec=p...]
    pmax x1 -> x0, blocking collectives: 38.9 us -> none  [merged(): row_best = lax.pmax(row_top, 'hits')]
    ppermute x0 -> x30, waiting for transfers between devices: none -> 37.7 us  [the longest x12 25.4 us: make_shards(): right = lambda x: lax.ppermute(x, 'hits', fwd)]
    ppermute x0 -> x30, starting transfers between devices: none -> 27.1 us  [the longest x12 21.3 us: make_shards(): right = lambda x: lax.ppermute(x, 'hits', fwd)]
    psum x1 -> x0, waiting for transfers between devices: 26.7 us -> none  [shards(): summed_units = lax.psum(partial_units, 'heads')]
    dot_general x19 -> x21, matrix products: 49.5 us -> 28.5 us  [the longest x5 10.3 us: ffn(): jnp.dot(x[:, fh:], up_oth, preferred_element_type=F32)]
  transfers between devices with their start and end apart: 6 -> 30, of which waited for: 6 -> 15; matrix products, arithmetic and copies ran while one was open for 1% -> 17% of each run, Pallas kernels for 0% -> 17%
where the time goes in v1:
time: 143 us
  Pallas kernels  39.1 us (27%)
  waiting for transfers between devices  37.7 us (26%)
  matrix products  28.5 us (20%)
  starting transfers between devices  27.1 us (19%)
  local copies, waits for them, and re-layouts  4.97 us (3%)
  other arithmetic  4.12 us (3%)
    pallas_call x5, Pallas kernels, attend(): pl.pallas_call(functools.partial(attn_kernel, heads, blocks), grid_spec=p...  28.4 us
    ppermute x12, waiting for transfers between devices, make_shards(): right = lambda x: lax.ppermute(x, 'hits', fwd)  25.4 us
    ppermute x12, starting transfers between devices, make_shards(): right = lambda x: lax.ppermute(x, 'hits', fwd)  21.3 us
    ppermute x12, waiting for transfers between devices, make_shards(): left = lambda x: lax.ppermute(x, 'hits', bwd)  10.9 us
    dot_general x5, matrix products, ffn(): jnp.dot(x[:, fh:], up_oth, preferred_element_type=F32)  10.3 us
    dot_general x5, matrix products, ffn(): jnp.dot(hid, down_oth, preferred_element_type=F32)  10.2 us
    pallas_call x4, Pallas kernels, merge(): pl.pallas_call(functools.partial(merge_kernel, heads, jobs, 0, rows), out...  8.48 us
    ppermute x12, starting transfers between devices, make_shards(): left = lambda x: lax.ppermute(x, 'hits', bwd)  4.6 us
  transfers between devices with their start and end apart: 30, of which 15 were waited for; matrix products, arithmetic and copies ran while one was open for 17% of the time, Pallas kernels for 17%

profile of v1, /device:TPU:0, one launch (start us, length us, event | category | flops | bytes accessed | tf_op | source)
XLA Modules:
  0.0 142.6 jit_solution(2968602977600559686)
XLA Ops:
  0.7 3.8 %attend.9 = (f32[1024,128]{1,0:T(8,128)}, f32[16,128]{1,0:T(8,128)}) custom-call(s32[1]{0:T(128)} %bitcast.7.idx_ref, s32[1]{0:T(128)S(6)} %copy.14.cnt_ref, bf16[1024,1024]{1,0:T(8,128)(2,1)} %refs_0_.9, bf16[512,1024]{1,0:T(8,128)(2,1)} %refs_1_.9, bf16[512,1024]{1,0:T(8,128)(2,1)} %refs_2_.9), custom_call_target="tpu_custom_call" | custom-call | flops 268435456 | bytes 2883584 | tf_op jit(solution)/shard_map/attend/pallas_call | solution.py:50
  4.4 1.8 %merge.4 = (bf16[528,128]{1,0:T(8,128)(2,1)}, bf16[528,128]{1,0:T(8,128)(2,1)}) custom-call(f32[1024,128]{1,0:T(8,128)} %get-tuple-element.31.refs_0_, f32[16,128]{1,0:T(8,128)} %get-tuple-element.32.refs_1_), custom_call_target="tpu_custom_call" | custom-call | flops 1081344 | bytes 1081344 | tf_op jit(solution)/shard_map/merge/pallas_call | solution.py:127
  6.2 3.1 %collective-permute-start.1 = (bf16[528,128]{1,0:T(8,128)(2,1)}, bf16[528,128]{1,0:T(8,128)(2,1)S(1)}, u32[]{:S(2)}, u32[]{:S(2)}) collective-permute-start(bf16[528,128]{1,0:T(8,128)(2,1)} %get-tuple-element.33), channel_id=1, source_target_pairs={{0,4},{4,8},{8,12},{12,14},{14,10},{10,6},{6,2},{2,0},{1,5},{5,9},... | collective-permute-start | bytes 405512 | tf_op jit(solution)/shard_map/ppermute | solution.py:178
  9.8 7.0 %attend.8 = (f32[1024,256]{1,0:T(8,128)}, f32[16,256]{1,0:T(8,128)}) custom-call(s32[2]{0:T(128)} %pad_add_fusion.2.idx_ref, s32[1]{0:T(128)S(6)} %copy.14.cnt_ref, bf16[1024,1024]{1,0:T(8,128)(2,1)} %refs_0_.9, bf16[1024,1024]{1,0:T(8,128)(2,1)} %refs_0_.9, bf16[512,1024]{1,0:T(8,128)(2,1)} %refs_1_.9, bf16[512,1024]{1,0:T(8,128)(2,1)} %refs_2_.9), custom_call_target="tpu_custom_call" | custom-call | flops 536870912 | bytes 3670016 | tf_op jit(solution)/shard_map/attend/pallas_call | solution.py:50
  17.5 2.1 %merge.5 = (bf16[1056,128]{1,0:T(8,128)(2,1)}, bf16[1056,128]{1,0:T(8,128)(2,1)}) custom-call(f32[1024,256]{1,0:T(8,128)} %get-tuple-element.29.refs_0_, f32[16,256]{1,0:T(8,128)} %get-tuple-element.30.refs_1_, bf16[528,128]{1,0:T(8,128)(2,1)} %copy-done.8, bf16[528,128]{1,0:T(8,128)(2,1)} %copy-done.9), custom_call_target="tpu_custom_call" | custom-call | flops 2162688 | bytes 2162688 | tf_op jit(solution)/shard_map/merge/pallas_call | solution.py:127
  19.6 2.0 %collective-permute-start.3 = (bf16[1056,128]{1,0:T(8,128)(2,1)}, bf16[1056,128]{1,0:T(8,128)(2,1)S(1)}, u32[]{:S(2)}, u32[]{:S(2)}) collective-permute-start(bf16[1056,128]{1,0:T(8,128)(2,1)} %get-tuple-element.35), channel_id=1, source_target_pairs={{0,4},{4,8},{8,12},{12,14},{14,10},{10,6},{6,2},{2,0},{1,5},{5,9},... | collective-permute-start | bytes 811016 | tf_op jit(solution)/shard_map/ppermute | solution.py:178
  22.3 7.0 %attend.7 = (f32[1024,256]{1,0:T(8,128)}, f32[16,256]{1,0:T(8,128)}) custom-call(s32[2]{0:T(128)} %get-tuple-element.58.idx_ref, s32[1]{0:T(128)S(6)} %copy.14.cnt_ref, bf16[1024,1024]{1,0:T(8,128)(2,1)} %refs_0_.9, bf16[1024,1024]{1,0:T(8,128)(2,1)} %refs_0_.9, bf16[512,1024]{1,0:T(8,128)(2,1)} %refs_1_.9, bf16[512,1024]{1,0:T(8,128)(2,1)} %refs_2_.9), custom_call_target="tpu_custom_call" | custom-call | flops 536870912 | bytes 3670016 | tf_op jit(solution)/shard_map/attend/pallas_call | solution.py:50
  30.1 2.3 %merge.6 = (bf16[1056,128]{1,0:T(8,128)(2,1)}, bf16[1056,128]{1,0:T(8,128)(2,1)}) custom-call(f32[1024,256]{1,0:T(8,128)} %get-tuple-element.27.refs_0_, f32[16,256]{1,0:T(8,128)} %get-tuple-element.28.refs_1_, bf16[1056,128]{1,0:T(8,128)(2,1)} %copy-done.2, bf16[1056,128]{1,0:T(8,128)(2,1)} %copy-done.3), custom_call_target="tpu_custom_call" | custom-call | flops 2162688 | bytes 2162688 | tf_op jit(solution)/shard_map/merge/pallas_call | solution.py:127
  32.4 2.0 %collective-permute-start.5 = (bf16[1056,128]{1,0:T(8,128)(2,1)}, bf16[1056,128]{1,0:T(8,128)(2,1)S(1)}, u32[]{:S(2)}, u32[]{:S(2)}) collective-permute-start(bf16[1056,128]{1,0:T(8,128)(2,1)} %get-tuple-element.37), channel_id=1, source_target_pairs={{0,4},{4,8},{8,12},{12,14},{14,10},{10,6},{6,2},{2,0},{1,5},{5,9},... | collective-permute-start | bytes 811016 | tf_op jit(solution)/shard_map/ppermute | solution.py:178
  34.4 7.0 %attend.6 = (f32[1024,256]{1,0:T(8,128)}, f32[16,256]{1,0:T(8,128)}) custom-call(s32[2]{0:T(128)} %get-tuple-element.57.idx_ref, s32[1]{0:T(128)S(6)} %copy.14.cnt_ref, bf16[1024,1024]{1,0:T(8,128)(2,1)} %refs_0_.9, bf16[1024,1024]{1,0:T(8,128)(2,1)} %refs_0_.9, bf16[512,1024]{1,0:T(8,128)(2,1)} %refs_1_.9, bf16[512,1024]{1,0:T(8,128)(2,1)} %refs_2_.9), custom_call_target="tpu_custom_call" | custom-call | flops 536870912 | bytes 3670016 | tf_op jit(solution)/shard_map/attend/pallas_call | solution.py:50
  42.2 2.3 %merge.7 = (bf16[1056,128]{1,0:T(8,128)(2,1)}, bf16[1056,128]{1,0:T(8,128)(2,1)}) custom-call(f32[1024,256]{1,0:T(8,128)} %get-tuple-element.25.refs_0_, f32[16,256]{1,0:T(8,128)} %get-tuple-element.26.refs_1_, bf16[1056,128]{1,0:T(8,128)(2,1)} %copy-done.4, bf16[1056,128]{1,0:T(8,128)(2,1)} %copy-done.5), custom_call_target="tpu_custom_call" | custom-call | flops 2162688 | bytes 2162688 | tf_op jit(solution)/shard_map/merge/pallas_call | solution.py:127
  44.5 2.0 %collective-permute-start.7 = (bf16[1056,128]{1,0:T(8,128)(2,1)}, bf16[1056,128]{1,0:T(8,128)(2,1)S(1)}, u32[]{:S(2)}, u32[]{:S(2)}) collective-permute-start(bf16[1056,128]{1,0:T(8,128)(2,1)} %get-tuple-element.39), channel_id=1, source_target_pairs={{0,4},{4,8},{8,12},{12,14},{14,10},{10,6},{6,2},{2,0},{1,5},{5,9},... | collective-permute-start | bytes 811016 | tf_op jit(solution)/shard_map/ppermute | solution.py:178
  46.5 3.8 %attend.5 = (f32[1024,128]{1,0:T(8,128)}, f32[16,128]{1,0:T(8,128)}) custom-call(s32[1]{0:T(128)} %bitcast.idx_ref, s32[1]{0:T(128)S(6)} %copy.14.cnt_ref, bf16[1024,1024]{1,0:T(8,128)(2,1)} %refs_0_.9, bf16[512,1024]{1,0:T(8,128)(2,1)} %refs_1_.9, bf16[512,1024]{1,0:T(8,128)(2,1)} %refs_2_.9), custom_call_target="tpu_custom_call" | custom-call | flops 268435456 | bytes 2883584 | tf_op jit(solution)/shard_map/attend/pallas_call | solution.py:50
  50.3 1.2 collective-permute-done.7.a_ref
  51.5 1.7 %collective-permute-done.8.b_ref = bf16[1056,128]{1,0:T(8,128)(2,1)S(1)} collective-permute-done((bf16[1056,128]{1,0:T(8,128)(2,1)}, bf16[1056,128]{1,0:T(8,128)(2,1)S(1)}, u32[]{:S(2)}, u32[]{:S(2)}) %collective-permute-start.8) | collective-permute-done | bytes 270368 | tf_op jit(solution)/shard_map/ppermute | solution.py:179
  53.9 2.2 %finish.1 = bf16[128,1024]{1,0:T(8,128)(2,1)} custom-call(f32[1024,128]{1,0:T(8,128)} %get-tuple-element.23.ctx_ref, f32[16,128]{1,0:T(8,128)} %get-tuple-element.24.st_ref, bf16[1056,128]{1,0:T(8,128)(2,1)} %copy-done.6, bf16[1056,128]{1,0:T(8,128)(2,1)} %copy-done.7), custom_call_target="tpu_custom_call" | custom-call | flops 1048576 | bytes 1310720 | tf_op jit(solution)/shard_map/finish/pallas_call | solution.py:161
  56.1 3.1 %fusion.78 = f32[128,2048]{1,0:T(8,128)S(1)} fusion(bf16[128,1024]{1,0:T(8,128)(2,1)} %finish.1, bf16[1024,2048]{1,0:T(8,128)(2,1)} %param.14), kind=kOutput, calls=%fused_computation.130 | convolution fusion | flops 536870912 | bytes 5505024 | tf_op jit(solution)/shard_map/dot_general | solution.py:225
  60.6 1.0 constant_dynamic-slice_fusion.2
  62.3 1.3 dynamic-slice_add_fusion
  64.1 1.9 %collective-permute-start.13 = (bf16[64,2048]{1,0:T(8,128)(2,1)S(1)}, bf16[64,2048]{1,0:T(8,128)(2,1)S(1)}, u32[]{:S(2)}, u32[]{:S(2)}) collective-permute-start(bf16[64,2048]{1,0:T(8,128)(2,1)S(1)} %multiply_convert_fusion), channel_id=1, source_target_pairs={{0,4},{4,8},{8,12},{12,14},{14,10},{10,6},{6,2},{2,0},{1,5},{5,9},... | collective-permute-start | bytes 786440 | tf_op jit(solution)/shard_map/ppermute | solution.py:178
  66.5 6.1 %collective-permute-done.13 = bf16[64,2048]{1,0:T(8,128)(2,1)S(1)} collective-permute-done((bf16[64,2048]{1,0:T(8,128)(2,1)S(1)}, bf16[64,2048]{1,0:T(8,128)(2,1)S(1)}, u32[]{:S(2)}, u32[]{:S(2)}) %collective-permute-start.13) | collective-permute-done | bytes 262176 | tf_op jit(solution)/shard_map/ppermute | solution.py:178
  72.6 1.7 %collective-permute-start.15 = (bf16[64,2048]{1,0:T(8,128)(2,1)S(1)}, bf16[64,2048]{1,0:T(8,128)(2,1)S(1)}, u32[]{:S(2)}, u32[]{:S(2)}) collective-permute-start(bf16[64,2048]{1,0:T(8,128)(2,1)S(1)} %collective-permute-done.13), channel_id=1, source_target_pairs={{0,4},{4,8},{8,12},{12,14},{14,10},{10,6},{6,2},{2,0},{1,5},{5,9},... | collective-permute-start | bytes 786440 | tf_op jit(solution)/shard_map/ppermute | solution.py:178
  74.8 5.5 %collective-permute-done.15 = bf16[64,2048]{1,0:T(8,128)(2,1)S(1)} collective-permute-done((bf16[64,2048]{1,0:T(8,128)(2,1)S(1)}, bf16[64,2048]{1,0:T(8,128)(2,1)S(1)}, u32[]{:S(2)}, u32[]{:S(2)}) %collective-permute-start.15) | collective-permute-done | bytes 262176 | tf_op jit(solution)/shard_map/ppermute | solution.py:178
  80.3 1.4 %collective-permute-start.17 = (bf16[64,2048]{1,0:T(8,128)(2,1)S(1)}, bf16[64,2048]{1,0:T(8,128)(2,1)S(1)}, u32[]{:S(2)}, u32[]{:S(2)}) collective-permute-start(bf16[64,2048]{1,0:T(8,128)(2,1)S(1)} %collective-permute-done.15), channel_id=1, source_target_pairs={{0,4},{4,8},{8,12},{12,14},{14,10},{10,6},{6,2},{2,0},{1,5},{5,9},... | collective-permute-start | bytes 786440 | tf_op jit(solution)/shard_map/ppermute | solution.py:178
  82.4 2.0 %fusion.63 = f32[128,1024]{1,0:T(8,128)S(1)} fusion(bf16[1024,1024]{1,0:T(8,128)(2,1)} %collective-permute-done.11, bf16[128,2048]{1,0:T(8,128)(2,1)S(1)} %constant_dynamic-update-slice_fusion.2), kind=kOutput, calls=%fused_computation.91 | convolution fusion | flops 268435456 | bytes 2883584 | tf_op jit(solution)/shard_map/dot_general | solution.py:238
  85.4 2.0 %fusion.66 = f32[128,1024]{1,0:T(8,128)S(1)} fusion(bf16[1024,1024]{1,0:T(8,128)(2,1)} %collective-permute-done.11, bf16[128,2048]{1,0:T(8,128)(2,1)S(1)} %constant_dynamic-update-slice_fusion), kind=kOutput, calls=%fused_computation.94 | convolution fusion | flops 268435456 | bytes 2883584 | tf_op jit(solution)/shard_map/dot_general | solution.py:238
  88.5 2.0 %fusion.84 = f32[128,1024]{1,0:T(8,128)S(1)} fusion(bf16[128,1024]{1,0:T(8,128)(2,1)S(1)} %fusion.16, bf16[1024,1024]{1,0:T(8,128)(2,1)} %collective-permute-done.12), kind=kOutput, calls=%fused_computation.136 | convolution fusion | flops 268435456 | bytes 2883584 | tf_op jit(solution)/shard_map/dot_general | solution.py:245
  90.5 2.0 %fusion.82 = f32[128,1024]{1,0:T(8,128)S(1)} fusion(bf16[128,1024]{1,0:T(8,128)(2,1)S(1)} %fusion.8, bf16[1024,1024]{1,0:T(8,128)(2,1)} %collective-permute-done.12), kind=kOutput, calls=%fused_computation.134 | convolution fusion | flops 268435456 | bytes 2883584 | tf_op jit(solution)/shard_map/dot_general | solution.py:245
  92.6 1.4 %collective-permute-start.20 = (bf16[32,2048]{1,0:T(8,128)(2,1)S(1)}, bf16[32,2048]{1,0:T(8,128)(2,1)S(1)}, u32[]{:S(2)}, u32[]{:S(2)}) collective-permute-start(bf16[32,2048]{1,0:T(8,128)(2,1)S(1)} %slice.129), channel_id=1, source_target_pairs={{4,0},{8,4},{12,8},{14,12},{10,14},{6,10},{2,6},{0,2},{5,1},{9,5},... | collective-permute-start | bytes 393224 | tf_op jit(solution)/shard_map/ppermute | solution.py:179
  94.8 2.0 %fusion.60 = f32[128,1024]{1,0:T(8,128)S(1)} fusion(bf16[1024,1024]{1,0:T(8,128)(2,1)} %collective-permute-done.11, bf16[128,2048]{1,0:T(8,128)(2,1)S(1)} %constant_dynamic-update-slice_fusion.4), kind=kOutput, calls=%fused_computation.88 | convolution fusion | flops 268435456 | bytes 2883584 | tf_op jit(solution)/shard_map/dot_general | solution.py:238
  97.8 2.0 %fusion.86 = f32[128,1024]{1,0:T(8,128)S(1)} fusion(bf16[128,1024]{1,0:T(8,128)(2,1)S(1)} %fusion.24, bf16[1024,1024]{1,0:T(8,128)(2,1)} %collective-permute-done.12), kind=kOutput, calls=%fused_computation.138 | convolution fusion | flops 268435456 | bytes 2883584 | tf_op jit(solution)/shard_map/dot_general | solution.py:245
  100.0 2.1 %fusion.70 = f32[64,1024]{1,0:T(8,128)S(1)} fusion(bf16[1024,1024]{1,0:T(8,128)(2,1)} %collective-permute-done.11, bf16[64,2048]{1,0:T(8,128)(2,1)S(1)} %constant_dynamic-update-slice_fusion.6), kind=kOutput, calls=%fused_computation.106 | convolution fusion | flops 134217728 | bytes 2490368 | tf_op jit(solution)/shard_map/dot_general | solution.py:238
  103.1 2.1 %convolution_convert_fusion = bf16[64,1024]{1,0:T(8,128)(2,1)S(1)} fusion(bf16[64,1024]{1,0:T(8,128)(2,1)S(1)} %fusion.53, bf16[1024,1024]{1,0:T(8,128)(2,1)} %collective-permute-done.12), kind=kOutput, calls=%fused_computation.10 | convolution fusion | flops 134283264 | bytes 2359296 | tf_op jit(solution)/shard_map/dot_general | solution.py:245
  105.2 1.5 %collective-permute-start.21 = (bf16[32,2048]{1,0:T(8,128)(2,1)S(1)}, bf16[32,2048]{1,0:T(8,128)(2,1)S(1)}, u32[]{:S(2)}, u32[]{:S(2)}) collective-permute-start(bf16[32,2048]{1,0:T(8,128)(2,1)S(1)} %get-tuple-element.53), channel_id=1, source_target_pairs={{0,4},{4,8},{8,12},{12,14},{14,10},{10,6},{6,2},{2,0},{1,5},{5,9},... | collective-permute-start | bytes 393224 | tf_op jit(solution)/shard_map/ppermute | solution.py:178
  107.3 2.9 %collective-permute-done.21 = bf16[32,2048]{1,0:T(8,128)(2,1)S(1)} collective-permute-done((bf16[32,2048]{1,0:T(8,128)(2,1)S(1)}, bf16[32,2048]{1,0:T(8,128)(2,1)S(1)}, u32[]{:S(2)}, u32[]{:S(2)}) %collective-permute-start.21) | collective-permute-done | bytes 131104 | tf_op jit(solution)/shard_map/ppermute | solution.py:178
  110.2 2.9 %collective-permute-done.25 = bf16[32,2048]{1,0:T(8,128)(2,1)S(1)} collective-permute-done((bf16[32,2048]{1,0:T(8,128)(2,1)S(1)}, bf16[32,2048]{1,0:T(8,128)(2,1)S(1)}, u32[]{:S(2)}, u32[]{:S(2)}) %collective-permute-start.25) | collective-permute-done | bytes 131104 | tf_op jit(solution)/shard_map/ppermute | solution.py:179
  113.6 1.7 %collective-permute-start.22 = (bf16[64,2048]{1,0:T(8,128)(2,1)S(1)}, bf16[64,2048]{1,0:T(8,128)(2,1)S(1)}, u32[]{:S(2)}, u32[]{:S(2)}) collective-permute-start(bf16[64,2048]{1,0:T(8,128)(2,1)S(1)} %pad_maximum_fusion.3), channel_id=1, source_target_pairs={{0,4},{4,8},{8,12},{12,14},{14,10},{10,6},{6,2},{2,0},{1,5},{5,9},... | collective-permute-start | bytes 786440 | tf_op jit(solution)/shard_map/ppermute | solution.py:178
  115.3 2.1 %fusion.45 = bf16[64,1024]{1,0:T(8,128)(2,1)S(1)} fusion(f32[64,1024]{1,0:T(8,128)S(1)} %fusion.74, bf16[1024,1024]{1,0:T(8,128)(2,1)} %collective-permute-done.11, bf16[64,2048]{1,0:T(8,128)(2,1)S(1)} %multiply_convert_fusion), kind=kOutput, calls=%fused_computation.73 | convolution fusion | flops 134873088 | bytes 2621440 | tf_op jit(solution)/shard_map/dot_general | solution.py:238
  117.4 3.5 %collective-permute-done.26 = bf16[64,2048]{1,0:T(8,128)(2,1)S(1)} collective-permute-done((bf16[64,2048]{1,0:T(8,128)(2,1)S(1)}, bf16[64,2048]{1,0:T(8,128)(2,1)S(1)}, u32[]{:S(2)}, u32[]{:S(2)}) %collective-permute-start.26) | collective-permute-done | bytes 262176 | tf_op jit(solution)/shard_map/ppermute | solution.py:179
  120.8 1.7 %collective-permute-done.22 = bf16[64,2048]{1,0:T(8,128)(2,1)S(1)} collective-permute-done((bf16[64,2048]{1,0:T(8,128)(2,1)S(1)}, bf16[64,2048]{1,0:T(8,128)(2,1)S(1)}, u32[]{:S(2)}, u32[]{:S(2)}) %collective-permute-start.22) | collective-permute-done | bytes 262176 | tf_op jit(solution)/shard_map/ppermute | solution.py:178
  122.7 1.6 %collective-permute-start.23 = (bf16[64,2048]{1,0:T(8,128)(2,1)S(1)}, bf16[64,2048]{1,0:T(8,128)(2,1)S(1)}, u32[]{:S(2)}, u32[]{:S(2)}) collective-permute-start(bf16[64,2048]{1,0:T(8,128)(2,1)S(1)} %get-tuple-element.43), channel_id=1, source_target_pairs={{0,4},{4,8},{8,12},{12,14},{14,10},{10,6},{6,2},{2,0},{1,5},{5,9},... | collective-permute-start | bytes 786440 | tf_op jit(solution)/shard_map/ppermute | solution.py:178
  125.2 5.6 %collective-permute-done.23 = bf16[64,2048]{1,0:T(8,128)(2,1)S(1)} collective-permute-done((bf16[64,2048]{1,0:T(8,128)(2,1)S(1)}, bf16[64,2048]{1,0:T(8,128)(2,1)S(1)}, u32[]{:S(2)}, u32[]{:S(2)}) %collective-permute-start.23) | collective-permute-done | bytes 262176 | tf_op jit(solution)/shard_map/ppermute | solution.py:178
  130.8 1.3 collective-permute-done.27
  132.3 1.6 %collective-permute-start.24 = (bf16[64,2048]{1,0:T(8,128)(2,1)S(1)}, bf16[64,2048]{1,0:T(8,128)(2,1)S(1)}, u32[]{:S(2)}, u32[]{:S(2)}) collective-permute-start(bf16[64,2048]{1,0:T(8,128)(2,1)S(1)} %get-tuple-element.41), channel_id=1, source_target_pairs={{0,4},{4,8},{8,12},{12,14},{14,10},{10,6},{6,2},{2,0},{1,5},{5,9},... | collective-permute-start | bytes 786440 | tf_op jit(solution)/shard_map/ppermute | solution.py:178
  134.3 2.1 %fusion.80 = f32[64,1024]{1,0:T(8,128)S(1)} fusion(bf16[64,1024]{1,0:T(8,128)(2,1)S(1)} %fusion.45, bf16[1024,1024]{1,0:T(8,128)(2,1)} %collective-permute-done.12), kind=kOutput, calls=%fused_computation.132 | convolution fusion | flops 134217728 | bytes 2490368 | tf_op jit(solution)/shard_map/dot_general | solution.py:245
  136.4 2.3 %collective-permute-done.24 = bf16[64,2048]{1,0:T(8,128)(2,1)S(1)} collective-permute-done((bf16[64,2048]{1,0:T(8,128)(2,1)S(1)}, bf16[64,2048]{1,0:T(8,128)(2,1)S(1)}, u32[]{:S(2)}, u32[]{:S(2)}) %collective-permute-start.24) | collective-permute-done | bytes 262176 | tf_op jit(solution)/shard_map/ppermute | solution.py:178
  138.7 1.6 %collective-permute-done.28 = bf16[64,2048]{1,0:T(8,128)(2,1)S(1)} collective-permute-done((bf16[64,2048]{1,0:T(8,128)(2,1)S(1)}, bf16[64,2048]{1,0:T(8,128)(2,1)S(1)}, u32[]{:S(2)}, u32[]{:S(2)}) %collective-permute-start.28) | collective-permute-done | bytes 262176 | tf_op jit(solution)/shard_map/ppermute | solution.py:179
  140.5 1.3 collective-permute-done.29
  (96 shorter events, 17.0 us)
Async XLA Ops:
  6.2 10.6 %collective-permute-start.1 = (bf16[528,128]{1,0:T(8,128)(2,1)}, bf16[528,128]{1,0:T(8,128)(2,1)S(1)}, u32[]{:S(2)}, u32[]{:S(2)}) collective-permute-start(bf16[528,128]{1,0:T(8,128)(2,1)} %get-tuple-element.33), channel_id=1, source_target_pairs={{0,4},{4,8},{8,12},{12,14},{14,10},{10,6},{6,2},{2,0},{1,5},{5,9},... | collective-permute-start | bytes 405512 | tf_op jit(solution)/shard_map/ppermute | solution.py:178
  9.2 7.6 %collective-permute-start.2 = (bf16[528,128]{1,0:T(8,128)(2,1)}, bf16[528,128]{1,0:T(8,128)(2,1)S(1)}, u32[]{:S(2)}, u32[]{:S(2)}) collective-permute-start(bf16[528,128]{1,0:T(8,128)(2,1)} %get-tuple-element.34), channel_id=1, source_target_pairs={{4,0},{8,4},{12,8},{14,12},{10,14},{6,10},{2,6},{0,2},{5,1},{9,5},... | collective-permute-start | bytes 405512 | tf_op jit(solution)/shard_map/ppermute | solution.py:179
  16.8 0.7 copy-start.8
  16.8 0.7 copy-start.9
  19.6 9.6 %collective-permute-start.3 = (bf16[1056,128]{1,0:T(8,128)(2,1)}, bf16[1056,128]{1,0:T(8,128)(2,1)S(1)}, u32[]{:S(2)}, u32[]{:S(2)}) collective-permute-start(bf16[1056,128]{1,0:T(8,128)(2,1)} %get-tuple-element.35), channel_id=1, source_target_pairs={{0,4},{4,8},{8,12},{12,14},{14,10},{10,6},{6,2},{2,0},{1,5},{5,9},... | collective-permute-start | bytes 811016 | tf_op jit(solution)/shard_map/ppermute | solution.py:178
  21.7 7.6 %collective-permute-start.4 = (bf16[1056,128]{1,0:T(8,128)(2,1)}, bf16[1056,128]{1,0:T(8,128)(2,1)S(1)}, u32[]{:S(2)}, u32[]{:S(2)}) collective-permute-start(bf16[1056,128]{1,0:T(8,128)(2,1)} %get-tuple-element.36), channel_id=1, source_target_pairs={{4,0},{8,4},{12,8},{14,12},{10,14},{6,10},{2,6},{0,2},{5,1},{9,5},... | collective-permute-start | bytes 811016 | tf_op jit(solution)/shard_map/ppermute | solution.py:179
  29.3 0.7 copy-start.2
  29.3 0.8 copy-start.3
  32.4 9.0 %collective-permute-start.5 = (bf16[1056,128]{1,0:T(8,128)(2,1)}, bf16[1056,128]{1,0:T(8,128)(2,1)S(1)}, u32[]{:S(2)}, u32[]{:S(2)}) collective-permute-start(bf16[1056,128]{1,0:T(8,128)(2,1)} %get-tuple-element.37), channel_id=1, source_target_pairs={{0,4},{4,8},{8,12},{12,14},{14,10},{10,6},{6,2},{2,0},{1,5},{5,9},... | collective-permute-start | bytes 811016 | tf_op jit(solution)/shard_map/ppermute | solution.py:178
  34.4 7.0 %collective-permute-start.6 = (bf16[1056,128]{1,0:T(8,128)(2,1)}, bf16[1056,128]{1,0:T(8,128)(2,1)S(1)}, u32[]{:S(2)}, u32[]{:S(2)}) collective-permute-start(bf16[1056,128]{1,0:T(8,128)(2,1)} %get-tuple-element.38), channel_id=1, source_target_pairs={{4,0},{8,4},{12,8},{14,12},{10,14},{6,10},{2,6},{0,2},{5,1},{9,5},... | collective-permute-start | bytes 811016 | tf_op jit(solution)/shard_map/ppermute | solution.py:179
  41.4 0.7 copy-start.4
  41.5 0.7 copy-start.5
  44.5 7.0 %collective-permute-start.7 = (bf16[1056,128]{1,0:T(8,128)(2,1)}, bf16[1056,128]{1,0:T(8,128)(2,1)S(1)}, u32[]{:S(2)}, u32[]{:S(2)}) collective-permute-start(bf16[1056,128]{1,0:T(8,128)(2,1)} %get-tuple-element.39), channel_id=1, source_target_pairs={{0,4},{4,8},{8,12},{12,14},{14,10},{10,6},{6,2},{2,0},{1,5},{5,9},... | collective-permute-start | bytes 811016 | tf_op jit(solution)/shard_map/ppermute | solution.py:178
  46.5 6.7 %collective-permute-start.8 = (bf16[1056,128]{1,0:T(8,128)(2,1)}, bf16[1056,128]{1,0:T(8,128)(2,1)S(1)}, u32[]{:S(2)}, u32[]{:S(2)}) collective-permute-start(bf16[1056,128]{1,0:T(8,128)(2,1)} %get-tuple-element.40), channel_id=1, source_target_pairs={{4,0},{8,4},{12,8},{14,12},{10,14},{6,10},{2,6},{0,2},{5,1},{9,5},... | collective-permute-start | bytes 811016 | tf_op jit(solution)/shard_map/ppermute | solution.py:179
  51.5 1.7 %copy-start.6 = (bf16[1056,128]{1,0:T(8,128)(2,1)}, bf16[1056,128]{1,0:T(8,128)(2,1)S(1)}, u32[]{:S(2)}) copy-start(bf16[1056,128]{1,0:T(8,128)(2,1)S(1)} %collective-permute-done.7.a_ref) | copy-start | bytes 811012
  53.2 0.7 copy-start.7
  56.1 4.0 %copy-start.10 = (f32[1024]{0:T(1024)S(1)}, f32[1024]{0:T(1024)}, u32[]{:S(2)}) copy-start(f32[1024]{0:T(1024)} %param.15) | copy-start | bytes 12292
  56.1 6.1 %copy-start = (bf16[1024,1024]{1,0:T(8,128)(2,1)S(1)}, bf16[1024,1024]{1,0:T(8,128)(2,1)}, u32[]{:S(2)}) copy-start(bf16[1024,1024]{1,0:T(8,128)(2,1)} %param.17) | copy-start | bytes 6291460
  60.0 2.3 %collective-permute-start.9 = (f32[64,2048]{1,0:T(8,128)}, f32[64,2048]{1,0:T(8,128)}, u32[]{:S(2)}, u32[]{:S(2)}) collective-permute-start(f32[64,2048]{1,0:T(8,128)} %constant_dynamic-slice_fusion), channel_id=1, source_target_pairs={{0,1},{1,0},{2,3},{3,2},{4,5},{5,4},{6,7},{7,6},{8,9},{9,8},{10,11... | collective-permute-start | bytes 1572872 | tf_op jit(solution)/shard_map/ppermute | solution.py:180
  60.1 2.2 %collective-permute-start.10 = (f32[1,1024]{1,0:T(1,128)S(1)}, f32[1,1024]{1,0:T(1,128)S(1)}, u32[]{:S(2)}, u32[]{:S(2)}) collective-permute-start(f32[1,1024]{1,0:T(1,128)S(1)} %bitcast.43), channel_id=1, source_target_pairs={{0,1},{1,0},{2,3},{3,2},{4,5},{5,4},{6,7},{7,6},{8,9},{9,8},{10,11... | collective-permute-start | bytes 12296 | tf_op jit(solution)/shard_map/ppermute | solution.py:180
  61.6 2.1 %collective-permute-start = (bf16[64,1024]{1,0:T(8,128)(2,1)S(1)}, bf16[64,1024]{1,0:T(8,128)(2,1)S(1)}, u32[]{:S(2)}, u32[]{:S(2)}) collective-permute-start(bf16[64,1024]{1,0:T(8,128)(2,1)S(1)} %get-tuple-element.56), channel_id=1, source_target_pairs={{0,1},{1,0},{2,3},{3,2},{4,5},{5,4},{6,7},{7,6},{8,9},{9,8},{10,11... | collective-permute-start | bytes 393224 | tf_op jit(solution)/shard_map/ppermute | solution.py:180
  61.6 20.8 %collective-permute-start.11 = (bf16[1024,1024]{1,0:T(8,128)(2,1)}, bf16[1024,1024]{1,0:T(8,128)(2,1)}, u32[]{:S(2)}, u32[]{:S(2)}) collective-permute-start(bf16[1024,1024]{1,0:T(8,128)(2,1)} %param.16), channel_id=1, source_target_pairs={{0,1},{1,0},{2,3},{3,2},{4,5},{5,4},{6,7},{7,6},{8,9},{9,8},{10,11... | collective-permute-start | bytes 6291464 | tf_op jit(solution)/shard_map/ppermute | solution.py:180
  62.1 26.3 %collective-permute-start.12 = (bf16[1024,1024]{1,0:T(8,128)(2,1)S(1)}, bf16[1024,1024]{1,0:T(8,128)(2,1)}, u32[]{:S(2)}, u32[]{:S(2)}) collective-permute-start(bf16[1024,1024]{1,0:T(8,128)(2,1)S(1)} %copy-done), channel_id=1, source_target_pairs={{0,1},{1,0},{2,3},{3,2},{4,5},{5,4},{6,7},{7,6},{8,9},{9,8},{10,11... | collective-permute-start | bytes 6291464 | tf_op jit(solution)/shard_map/ppermute | solution.py:180
  62.3 3.7 %copy-start.1 = (bf16[1024,1024]{1,0:T(8,128)(2,1)S(1)}, bf16[1024,1024]{1,0:T(8,128)(2,1)}, u32[]{:S(2)}) copy-start(bf16[1024,1024]{1,0:T(8,128)(2,1)} %param.16) | copy-start | bytes 6291460
  64.0 10.4 %collective-permute-start.14 = (bf16[64,2048]{1,0:T(8,128)(2,1)S(1)}, bf16[64,2048]{1,0:T(8,128)(2,1)S(1)}, u32[]{:S(2)}, u32[]{:S(2)}) collective-permute-start(bf16[64,2048]{1,0:T(8,128)(2,1)S(1)} %multiply_convert_fusion), channel_id=1, source_target_pairs={{4,0},{8,4},{12,8},{14,12},{10,14},{6,10},{2,6},{0,2},{5,1},{9,5},... | collective-permute-start | bytes 786440 | tf_op jit(solution)/shard_map/ppermute | solution.py:179
  64.1 8.5 %collective-permute-start.13 = (bf16[64,2048]{1,0:T(8,128)(2,1)S(1)}, bf16[64,2048]{1,0:T(8,128)(2,1)S(1)}, u32[]{:S(2)}, u32[]{:S(2)}) collective-permute-start(bf16[64,2048]{1,0:T(8,128)(2,1)S(1)} %multiply_convert_fusion), channel_id=1, source_target_pairs={{0,4},{4,8},{8,12},{12,14},{14,10},{10,6},{6,2},{2,0},{1,5},{5,9},... | collective-permute-start | bytes 786440 | tf_op jit(solution)/shard_map/ppermute | solution.py:178
  72.6 7.6 %collective-permute-start.15 = (bf16[64,2048]{1,0:T(8,128)(2,1)S(1)}, bf16[64,2048]{1,0:T(8,128)(2,1)S(1)}, u32[]{:S(2)}, u32[]{:S(2)}) collective-permute-start(bf16[64,2048]{1,0:T(8,128)(2,1)S(1)} %collective-permute-done.13), channel_id=1, source_target_pairs={{0,4},{4,8},{8,12},{12,14},{14,10},{10,6},{6,2},{2,0},{1,5},{5,9},... | collective-permute-start | bytes 786440 | tf_op jit(solution)/shard_map/ppermute | solution.py:178
  74.3 7.4 %collective-permute-start.16 = (bf16[64,2048]{1,0:T(8,128)(2,1)S(1)}, bf16[64,2048]{1,0:T(8,128)(2,1)S(1)}, u32[]{:S(2)}, u32[]{:S(2)}) collective-permute-start(bf16[64,2048]{1,0:T(8,128)(2,1)S(1)} %collective-permute-done.14), channel_id=1, source_target_pairs={{4,0},{8,4},{12,8},{14,12},{10,14},{6,10},{2,6},{0,2},{5,1},{9,5},... | collective-permute-start | bytes 786440 | tf_op jit(solution)/shard_map/ppermute | solution.py:179
  80.3 13.7 %collective-permute-start.17 = (bf16[64,2048]{1,0:T(8,128)(2,1)S(1)}, bf16[64,2048]{1,0:T(8,128)(2,1)S(1)}, u32[]{:S(2)}, u32[]{:S(2)}) collective-permute-start(bf16[64,2048]{1,0:T(8,128)(2,1)S(1)} %collective-permute-done.15), channel_id=1, source_target_pairs={{0,4},{4,8},{8,12},{12,14},{14,10},{10,6},{6,2},{2,0},{1,5},{5,9},... | collective-permute-start | bytes 786440 | tf_op jit(solution)/shard_map/ppermute | solution.py:178
  81.8 10.8 %collective-permute-start.18 = (bf16[64,2048]{1,0:T(8,128)(2,1)S(1)}, bf16[64,2048]{1,0:T(8,128)(2,1)S(1)}, u32[]{:S(2)}, u32[]{:S(2)}) collective-permute-start(bf16[64,2048]{1,0:T(8,128)(2,1)S(1)} %collective-permute-done.16), channel_id=1, source_target_pairs={{4,0},{8,4},{12,8},{14,12},{10,14},{6,10},{2,6},{0,2},{5,1},{9,5},... | collective-permute-start | bytes 786440 | tf_op jit(solution)/shard_map/ppermute | solution.py:179
  92.6 7.4 %collective-permute-start.20 = (bf16[32,2048]{1,0:T(8,128)(2,1)S(1)}, bf16[32,2048]{1,0:T(8,128)(2,1)S(1)}, u32[]{:S(2)}, u32[]{:S(2)}) collective-permute-start(bf16[32,2048]{1,0:T(8,128)(2,1)S(1)} %slice.129), channel_id=1, source_target_pairs={{4,0},{8,4},{12,8},{14,12},{10,14},{6,10},{2,6},{0,2},{5,1},{9,5},... | collective-permute-start | bytes 393224 | tf_op jit(solution)/shard_map/ppermute | solution.py:179
  94.0 5.9 %collective-permute-start.19 = (bf16[32,2048]{1,0:T(8,128)(2,1)S(1)}, bf16[32,2048]{1,0:T(8,128)(2,1)S(1)}, u32[]{:S(2)}, u32[]{:S(2)}) collective-permute-start(bf16[32,2048]{1,0:T(8,128)(2,1)S(1)} %slice.128), channel_id=1, source_target_pairs={{0,4},{4,8},{8,12},{12,14},{14,10},{10,6},{6,2},{2,0},{1,5},{5,9},... | collective-permute-start | bytes 393224 | tf_op jit(solution)/shard_map/ppermute | solution.py:178
  105.2 5.0 %collective-permute-start.21 = (bf16[32,2048]{1,0:T(8,128)(2,1)S(1)}, bf16[32,2048]{1,0:T(8,128)(2,1)S(1)}, u32[]{:S(2)}, u32[]{:S(2)}) collective-permute-start(bf16[32,2048]{1,0:T(8,128)(2,1)S(1)} %get-tuple-element.53), channel_id=1, source_target_pairs={{0,4},{4,8},{8,12},{12,14},{14,10},{10,6},{6,2},{2,0},{1,5},{5,9},... | collective-permute-start | bytes 393224 | tf_op jit(solution)/shard_map/ppermute | solution.py:178
  106.7 6.4 %collective-permute-start.25 = (bf16[32,2048]{1,0:T(8,128)(2,1)S(1)}, bf16[32,2048]{1,0:T(8,128)(2,1)S(1)}, u32[]{:S(2)}, u32[]{:S(2)}) collective-permute-start(bf16[32,2048]{1,0:T(8,128)(2,1)S(1)} %get-tuple-element.54), channel_id=1, source_target_pairs={{4,0},{8,4},{12,8},{14,12},{10,14},{6,10},{2,6},{0,2},{5,1},{9,5},... | collective-permute-start | bytes 393224 | tf_op jit(solution)/shard_map/ppermute | solution.py:179
  113.1 7.7 %collective-permute-start.26 = (bf16[64,2048]{1,0:T(8,128)(2,1)S(1)}, bf16[64,2048]{1,0:T(8,128)(2,1)S(1)}, u32[]{:S(2)}, u32[]{:S(2)}) collective-permute-start(bf16[64,2048]{1,0:T(8,128)(2,1)S(1)} %pad_maximum_fusion.4), channel_id=1, source_target_pairs={{4,0},{8,4},{12,8},{14,12},{10,14},{6,10},{2,6},{0,2},{5,1},{9,5},... | collective-permute-start | bytes 786440 | tf_op jit(solution)/shard_map/ppermute | solution.py:179
  113.6 8.9 %collective-permute-start.22 = (bf16[64,2048]{1,0:T(8,128)(2,1)S(1)}, bf16[64,2048]{1,0:T(8,128)(2,1)S(1)}, u32[]{:S(2)}, u32[]{:S(2)}) collective-permute-start(bf16[64,2048]{1,0:T(8,128)(2,1)S(1)} %pad_maximum_fusion.3), channel_id=1, source_target_pairs={{0,4},{4,8},{8,12},{12,14},{14,10},{10,6},{6,2},{2,0},{1,5},{5,9},... | collective-permute-start | bytes 786440 | tf_op jit(solution)/shard_map/ppermute | solution.py:178
  122.7 8.2 %collective-permute-start.23 = (bf16[64,2048]{1,0:T(8,128)(2,1)S(1)}, bf16[64,2048]{1,0:T(8,128)(2,1)S(1)}, u32[]{:S(2)}, u32[]{:S(2)}) collective-permute-start(bf16[64,2048]{1,0:T(8,128)(2,1)S(1)} %get-tuple-element.43), channel_id=1, source_target_pairs={{0,4},{4,8},{8,12},{12,14},{14,10},{10,6},{6,2},{2,0},{1,5},{5,9},... | collective-permute-start | bytes 786440 | tf_op jit(solution)/shard_map/ppermute | solution.py:178
  124.3 7.8 %collective-permute-start.27 = (bf16[64,2048]{1,0:T(8,128)(2,1)S(1)}, bf16[64,2048]{1,0:T(8,128)(2,1)S(1)}, u32[]{:S(2)}, u32[]{:S(2)}) collective-permute-start(bf16[64,2048]{1,0:T(8,128)(2,1)S(1)} %get-tuple-element.44), channel_id=1, source_target_pairs={{4,0},{8,4},{12,8},{14,12},{10,14},{6,10},{2,6},{0,2},{5,1},{9,5},... | collective-permute-start | bytes 786440 | tf_op jit(solution)/shard_map/ppermute | solution.py:179
  132.3 6.4 %collective-permute-start.24 = (bf16[64,2048]{1,0:T(8,128)(2,1)S(1)}, bf16[64,2048]{1,0:T(8,128)(2,1)S(1)}, u32[]{:S(2)}, u32[]{:S(2)}) collective-permute-start(bf16[64,2048]{1,0:T(8,128)(2,1)S(1)} %get-tuple-element.41), channel_id=1, source_target_pairs={{0,4},{4,8},{8,12},{12,14},{14,10},{10,6},{6,2},{2,0},{1,5},{5,9},... | collective-permute-start | bytes 786440 | tf_op jit(solution)/shard_map/ppermute | solution.py:178
  133.9 6.4 %collective-permute-start.28 = (bf16[64,2048]{1,0:T(8,128)(2,1)S(1)}, bf16[64,2048]{1,0:T(8,128)(2,1)S(1)}, u32[]{:S(2)}, u32[]{:S(2)}) collective-permute-start(bf16[64,2048]{1,0:T(8,128)(2,1)S(1)} %get-tuple-element.42), channel_id=1, source_target_pairs={{4,0},{8,4},{12,8},{14,12},{10,14},{6,10},{2,6},{0,2},{5,1},{9,5},... | collective-permute-start | bytes 786440 | tf_op jit(solution)/shard_map/ppermute | solution.py:179
  140.4 1.4 collective-permute-start.29

commit v2 on v1

v2 whole, which is shorter than its diff:
```python
import functools
import math

import jax
import jax.numpy as jnp
from jax import lax
from jax.experimental import pallas as pl
from jax.experimental.pallas import tpu as pltpu
from jax.sharding import PartitionSpec as P

HD = 128
BF = jnp.bfloat16
F32 = jnp.float32
EXP_SCALE = math.log2(math.e) / math.sqrt(HD)
DEAD = -1e30


def turned(x):
    k, rows = x.shape
    if k < HD:
        x = jnp.concatenate([x, jnp.zeros((HD - k, rows), x.dtype)], axis=0)
    return jnp.transpose(x)


VMEM_LIMIT = 16 * 2**20
vmem = pl.BlockSpec(memory_space=pltpu.VMEM)
smem = pl.BlockSpec(memory_space=pltpu.SMEM)


def local_call(kernel, out_shape, in_specs, name, flops, nbytes, exps=0, scratch=()):
    return pl.pallas_call(
        kernel,
        out_shape=[pltpu.VMEM(s.shape, s.dtype) for s in out_shape],
        in_specs=in_specs,
        out_specs=[vmem] * len(out_shape),
        scratch_shapes=list(scratch),
        cost_estimate=pl.CostEstimate(flops=flops, bytes_accessed=nbytes, transcendentals=exps),
        compiler_params=pltpu.CompilerParams(vmem_limit_bytes=VMEM_LIMIT),
        name=name,
    )


def attn_kernel(heads, blocks, rows, idx_ref, cnt_ref, q_ref, k_ref, v_ref, ctx_ref, st_ref, qs, sem):
    hits = k_ref.shape[0]
    copies = [
        pltpu.make_async_copy(
            q_ref.at[pl.ds(pl.multiple_of(idx_ref[b] * rows, rows), rows), :],
            qs.at[pl.ds(b * rows, rows), :],
            sem.at[b],
        )
        for b in range(blocks)
    ]
    for c in copies:
        c.start()
    live = lax.broadcasted_iota(jnp.int32, (1, hits), 1) < cnt_ref[0]
    bias = jnp.where(live, 0.0, DEAD)
    ones_v = jnp.ones((hits, HD), BF)
    lane = lax.broadcasted_iota(jnp.int32, (blocks * rows, HD), 1)
    for c in copies:
        c.wait()

    def scores(h):
        cols = slice(h * HD, (h + 1) * HD)
        s = lax.dot_general(
            qs[:, cols], k_ref[:, cols], (((1,), (1,)), ((), ())), preferred_element_type=F32
        )
        return s + bias

    st = jnp.zeros((blocks * rows, HD), F32)
    ahead = scores(0)
    for h in range(heads):
        s = ahead
        if h + 1 < heads:
            ahead = scores(h + 1)
        top = jnp.max(s, axis=1, keepdims=True).astype(BF).astype(F32)
        p = jnp.exp2((s - top) * EXP_SCALE).astype(BF)
        o = jnp.dot(
            p,
            jnp.concatenate([v_ref[:, h * HD : (h + 1) * HD], ones_v], axis=1),
            preferred_element_type=F32,
        )
        for b in range(blocks):
            at = (b * heads + h) * rows
            ctx_ref[at : at + rows, :] = o[b * rows : (b + 1) * rows, :HD]
        st = jnp.where(lane == h, top, st)
        st = jnp.where(lane == heads + h, o[:, HD:], st)
    st_ref[...] = jnp.transpose(st)[: 2 * heads]


def attend(idx, cnt, q, k, v, rows):
    blocks = idx.shape[0]
    hits, width = k.shape
    heads = width // HD
    n = blocks * rows
    return local_call(
        functools.partial(attn_kernel, heads, blocks, rows),
        [jax.ShapeDtypeStruct((n * heads, HD), F32), jax.ShapeDtypeStruct((2 * heads, n), F32)],
        [smem, smem, pl.BlockSpec(memory_space=pl.ANY), vmem, vmem],
        "attend",
        4 * n * hits * width,
        n * width * 6,
        n * hits * heads,
        [pltpu.VMEM((n, width), BF), pltpu.SemaphoreType.DMA((blocks,))],
    )(idx, cnt, q, k, v)


def group_rows(gh, rows):
    return gh * rows + 4 * gh


def read_group(msg_ref, base, gh, rows):
    st = msg_ref[base + gh * rows : base + gh * rows + 4 * gh, :rows].astype(F32)
    return st[:gh], st[gh : 2 * gh] + st[2 * gh : 3 * gh]


def write_stats(out_ref, base, gh, rows, top, total):
    hi = total.astype(BF).astype(F32)
    st = jnp.concatenate([top, hi, total - hi, jnp.zeros_like(top)], axis=0).astype(BF)
    if rows < HD:
        st = jnp.concatenate([st, jnp.zeros((4 * gh, HD - rows), BF)], axis=1)
    out_ref[base + gh * rows : base + gh * rows + 4 * gh, :] = st


def merge_kernel(heads, jobs, rows, *refs):
    gh = heads // 2
    gr = group_rows(gh, rows)
    ctx_ref, st_ref = refs[0], refs[1]
    n_msg = sum(1 for j in jobs if j[2])
    msgs, outs = refs[2 : 2 + n_msg], refs[2 + n_msg :]
    at = 0
    for (b, groups, held), out_ref in zip(jobs, outs):
        cols = slice(b * rows, (b + 1) * rows)
        msg_ref = None
        if held:
            msg_ref = msgs[at]
            at += 1
        for g in groups:
            base = groups.index(g) * gr
            own = (b * heads + g * gh) * rows
            top = st_ref[g * gh : (g + 1) * gh, cols]
            total = st_ref[heads + g * gh : heads + (g + 1) * gh, cols]
            if g in held:
                mbase = held.index(g) * gr
                mtop, mtotal = read_group(msg_ref, mbase, gh, rows)
                best = jnp.maximum(top, mtop)
                fa = jnp.exp2((top - best) * EXP_SCALE)
                fb = jnp.exp2((mtop - best) * EXP_SCALE)
                f = turned(jnp.concatenate([fa, fb], axis=0))
                for h in range(gh):
                    out_ref[base + h * rows : base + (h + 1) * rows, :] = (
                        ctx_ref[own + h * rows : own + (h + 1) * rows, :] * f[:, h : h + 1]
                        + msg_ref[mbase + h * rows : mbase + (h + 1) * rows, :].astype(F32)
                        * f[:, gh + h : gh + h + 1]
                    ).astype(BF)
                write_stats(out_ref, base, gh, rows, best, total * fa + mtotal * fb)
            else:
                out_ref[base : base + gh * rows, :] = ctx_ref[own : own + gh * rows, :].astype(BF)
                write_stats(out_ref, base, gh, rows, top, total)


def merge(ctx, st, msgs, jobs, heads, rows):
    gr = group_rows(heads // 2, rows)
    outs = [jax.ShapeDtypeStruct((len(j[1]) * gr, HD), BF) for j in jobs]
    nbytes = sum(len(j[1]) * gr * HD * 8 for j in jobs)
    return local_call(
        functools.partial(merge_kernel, heads, jobs, rows),
        outs,
        [vmem] * (2 + len(msgs)),
        "merge",
        nbytes,
        nbytes,
    )(ctx, st, *msgs)


def project_kernel(heads, rows, core_ref, ctx_ref, st_ref, a_ref, b_ref, w_ref, mine_ref, theirs_ref, ctx_s):
    gh = heads // 2
    gr = group_rows(gh, rows)
    for g in range(2):
        top = st_ref[g * gh : (g + 1) * gh, :]
        total = st_ref[heads + g * gh : heads + (g + 1) * gh, :]
        atop, atotal = read_group(a_ref, g * gr, gh, rows)
        btop, btotal = read_group(b_ref, g * gr, gh, rows)
        best = jnp.maximum(jnp.maximum(top, atop), btop)
        f0 = jnp.exp2((top - best) * EXP_SCALE)
        fa = jnp.exp2((atop - best) * EXP_SCALE)
        fb = jnp.exp2((btop - best) * EXP_SCALE)
        total = total * f0 + atotal * fa + btotal * fb
        f = turned(jnp.concatenate([f0 / total, fa / total, fb / total], axis=0))
        for h in range(gh):
            own = slice((g * gh + h) * rows, (g * gh + h + 1) * rows)
            far = slice(g * gr + h * rows, g * gr + (h + 1) * rows)
            ctx_s[:, (g * gh + h) * HD : (g * gh + h + 1) * HD] = (
                ctx_ref[own, :] * f[:, h : h + 1]
                + a_ref[far, :].astype(F32) * f[:, gh + h : gh + h + 1]
                + b_ref[far, :].astype(F32) * f[:, 2 * gh + h : 2 * gh + h + 1]
            ).astype(BF)
    mine, fh = rows // 2, w_ref.shape[1] // 2
    core = core_ref[0]
    keep = pl.ds(pl.multiple_of(core * mine, mine), mine)
    give = pl.ds(pl.multiple_of((1 - core) * mine, mine), mine)
    near = pl.ds(pl.multiple_of(core * fh, fh), fh)
    away = pl.ds(pl.multiple_of((1 - core) * fh, fh), fh)
    both = jnp.concatenate([ctx_s[keep, :], ctx_s[give, :]], axis=0)
    for cols, here, there in ((near, 0, 1), (away, 1, 0)):
        y = jnp.dot(both, w_ref[:, cols], preferred_element_type=F32)
        mine_ref[:, here * fh : (here + 1) * fh] = y[:mine]
        theirs_ref[:, there * fh : (there + 1) * fh] = y[mine:]


def project(core, ctx, st, a, b, w, heads, rows):
    out = jax.ShapeDtypeStruct((rows // 2, w.shape[1]), F32)
    return local_call(
        functools.partial(project_kernel, heads, rows),
        [out, out],
        [smem] + [vmem] * 5,
        "project",
        2 * rows * w.size,
        rows * heads * HD * 10 + w.size * 2,
        0,
        [pltpu.VMEM((rows, heads * HD), BF)],
    )(core, ctx, st, a, b, w)


def norm_kernel(mine_ref, theirs_ref, la_ref, lb_ref, ga_ref, gb_ref, stream_ref, normed_ref):
    fh = la_ref.shape[1]
    x = [
        mine_ref[:, c] + theirs_ref[:, c] + l[...].astype(F32)
        for c, l in ((slice(0, fh), la_ref), (slice(fh, 2 * fh), lb_ref))
    ]
    squares = sum(jnp.sum(v * v, axis=1, keepdims=True) for v in x) / (2 * fh)
    scale = lax.rsqrt(squares + 1e-06)
    for i, g in enumerate((ga_ref, gb_ref)):
        stream_ref[:, i * fh : (i + 1) * fh] = x[i]
        normed_ref[:, i * fh : (i + 1) * fh] = (x[i] * scale * g[...]).astype(BF)


def ffn_kernel(m, *refs):
    xs, (ua, ub, da, db), outs = refs[:m], refs[m : m + 4], refs[m + 4 :]
    fh = ua.shape[0]
    x = xs[0][...] if m == 1 else jnp.concatenate([r[...] for r in xs], axis=0)
    pre = jnp.dot(x[:, :fh], ua[...], preferred_element_type=F32)
    pre += jnp.dot(x[:, fh:], ub[...], preferred_element_type=F32)
    hid = jax.nn.gelu(pre).astype(BF)
    for i, w in enumerate((da, db)):
        y = jnp.dot(hid, w[...], preferred_element_type=F32)
        at = 0
        for r, o in zip(xs, outs):
            o[:, i * fh : (i + 1) * fh] = y[at : at + r.shape[0]].astype(o.dtype)
            at += r.shape[0]


def ffn(xs, weights, dtype):
    size = sum(w.size for w in weights)
    m = sum(x.shape[0] for x in xs)
    return local_call(
        functools.partial(ffn_kernel, len(xs)),
        [jax.ShapeDtypeStruct(x.shape, dtype) for x in xs],
        [vmem] * (len(xs) + 4),
        "ffn",
        2 * m * size,
        2 * size,
        m * weights[0].shape[1],
    )(*xs, *weights)


def make_shards(n):
    half = n // 2
    order = list(range(0, n, 2)) + list(range(n - 1, 0, -2))
    fwd = [(order[i], order[(i + 1) % n]) for i in range(n)]
    bwd = [(b, a) for a, b in fwd]
    swap = [(0, 1), (1, 0)]

    right = lambda x: lax.ppermute(x, "hits", fwd)
    left = lambda x: lax.ppermute(x, "hits", bwd)
    partner = lambda x: lax.ppermute(x, "heads", swap)

    def shards(queries, keys, values, hit_counts, latents, out_proj, norm_gain, up_proj, down_proj):
        core = lax.axis_index("heads")
        me = lax.axis_index("hits")
        pos = jnp.where(me % 2 == 0, me // 2, n - 1 - me // 2)

        def block_at(k):
            p = lax.rem(pos + (k + n), n)
            return jnp.where(p < half, 2 * p, 2 * (n - 1 - p) + 1)

        rows = latents.shape[0]
        mine = rows // 2
        width = keys.shape[1]
        heads = width // HD
        feats = 2 * latents.shape[1]
        fh = latents.shape[1]
        cnt = hit_counts.astype(jnp.int32)

        up_oth = partner(up_proj)
        down_oth = partner(down_proj)
        gain_own = norm_gain.reshape(1, fh)
        gain_oth = partner(gain_own)
        lat_own = lax.dynamic_slice_in_dim(latents, core * mine, mine, 0)
        lat_oth = partner(lax.dynamic_slice_in_dim(latents, (1 - core) * mine, mine, 0))

        def partial(ks):
            idx = jnp.stack([block_at(k) for k in ks]).astype(jnp.int32)
            return attend(idx, cnt, queries, keys, values, rows)

        ctx, st = partial([half])
        msg_r, msg_l = merge(ctx, st, [], ((0, (0,), ()), (0, (1,), ())), heads, rows)
        held_r, held_l = (0,), (1,)
        for t in range(2, half + 1):
            msg_r, msg_l = right(msg_r), left(msg_l)
            ctx, st = partial([half - t + 1, t - 1 - half])
            msg_r, msg_l = merge(
                ctx, st, [msg_r, msg_l], ((0, (0, 1), held_r), (1, (0, 1), held_l)), heads, rows
            )
            held_r = held_l = (0, 1)
        msg_r, msg_l = right(msg_r), left(msg_l)
        ctx, st = partial([0])
        core_id = core.reshape(1).astype(jnp.int32)
        proj, proj_oth = project(core_id, ctx, st, msg_r, msg_l, out_proj, heads, rows)
        proj_oth = partner(proj_oth)
        stream, normed = local_call(
            norm_kernel,
            [jax.ShapeDtypeStruct((mine, feats), F32), jax.ShapeDtypeStruct((mine, feats), BF)],
            [vmem] * 6,
            "norm",
            mine * feats * 8,
            mine * feats * 18,
        )(proj, proj_oth, lat_own, lat_oth, gain_own, gain_oth)
        weights = (up_proj, up_oth, down_proj, down_oth)

        hm = mine // 2
        from_l, from_r = normed, normed
        outs = {}
        for s in range(1, half):
            from_l, from_r = right(from_l), left(from_r)
            outs[-s], outs[s] = ffn([from_l, from_r], weights, F32)
        last_l, last_r = right(from_l[:hm]), left(from_r[hm:])
        far_r, far_l = ffn([last_l, last_r], weights, BF)
        own = ffn([normed], weights, F32)[0]

        msg_r, msg_l = right(far_r), left(far_l)
        for t in range(2, half + 1):
            a, b = outs[half - t + 1], outs[t - 1 - half]
            if t == 2:
                a = jnp.concatenate([a[:hm] + msg_r.astype(F32), a[hm:]], axis=0)
                b = jnp.concatenate([b[:hm], b[hm:] + msg_l.astype(F32)], axis=0)
            else:
                a, b = a + msg_r.astype(F32), b + msg_l.astype(F32)
            msg_r, msg_l = right(a.astype(BF)), left(b.astype(BF))
        total = stream + own + msg_r.astype(F32) + msg_l.astype(F32)
        total = total.astype(BF)
        keep, give = total[:, :fh], partner(total[:, fh:])
        return jnp.where(
            core == 0,
            jnp.concatenate([keep, give], axis=0),
            jnp.concatenate([give, keep], axis=0),
        )

    return shards


def solution(mesh):
    return jax.shard_map(
        make_shards(mesh.shape["hits"]),
        mesh=mesh,
        in_specs=(
            P("groups", "heads"),
            P(("groups", "hits"), "heads"),
            P(("groups", "hits"), "heads"),
            P(("groups", "hits")),
            P(("groups", "hits"), "heads"),
            P("heads", None),
            P("heads"),
            P("heads", "hits"),
            P("hits", "heads"),
        ),
        out_specs=P(("groups", "hits"), "heads"),
        check_vma=False,
    )
```

time: 143 us -> 130 us (0.909)
  matrix products: 28.5 us -> 0 us
  waiting for transfers between devices: 37.7 us -> 48 us
  local copies, waits for them, and re-layouts: 4.97 us -> 9.05 us
  Pallas kernels: 39.1 us -> 43 us
  other arithmetic: 4.12 us -> 1.39 us
    dot_general x21 -> x0, matrix products: 28.5 us -> none  [the longest x5 10.3 us: ffn(): jnp.dot(x[:, fh:], up_oth, preferred_element_type=F32)]
    ppermute x12, waiting for transfers between devices: 10.9 us -> 19.6 us  [make_shards(): left = lambda x: lax.ppermute(x, 'hits', bwd)]
    unnamed x26 -> x24, local copies, waits for them, and re-layouts: 3.01 us -> 8.95 us
    ppermute x12, starting transfers between devices: 4.6 us -> 9.88 us  [make_shards(): left = lambda x: lax.ppermute(x, 'hits', bwd)]
    ppermute x12, starting transfers between devices: 21.3 us -> 16.2 us  [make_shards(): right = lambda x: lax.ppermute(x, 'hits', fwd)]
    pallas_call x10 -> x16, Pallas kernels: 39.1 us -> 43 us  [the longest x5 24.7 us: ffn(): local_call(functools.partial(ffn_kernel, len(xs)), [jax.ShapeDtypeStruct(...]
    dynamic_slice x2 -> x1, local copies, waits for them, and re-layouts: 1.84 us -> 0.02 us  [shards(): lax.dynamic_slice_in_dim(latents, (1 - core) * mine, mine, 0)]
  transfers between devices with their start and end apart: 30 -> 30, of which waited for: 15 -> 19; matrix products, arithmetic and copies ran while one was open for 17% -> 0% of each run, Pallas kernels for 17% -> 27%
where the time goes in v2:
time: 130 us
  waiting for transfers between devices  48 us (37%)
  Pallas kernels  43 us (33%)
  starting transfers between devices  27.4 us (21%)
  local copies, waits for them, and re-layouts  9.05 us (7%)
  other arithmetic  1.39 us (1%)
    ppermute x12, waiting for transfers between devices, make_shards(): right = lambda x: lax.ppermute(x, 'hits', fwd)  25.7 us
    pallas_call x5, Pallas kernels, ffn(): local_call(functools.partial(ffn_kernel, len(xs)), [jax.ShapeDtypeStruct(...  24.7 us
    ppermute x12, waiting for transfers between devices, make_shards(): left = lambda x: lax.ppermute(x, 'hits', bwd)  19.6 us
    ppermute x12, starting transfers between devices, make_shards(): right = lambda x: lax.ppermute(x, 'hits', fwd)  16.2 us
    ppermute x12, starting transfers between devices, make_shards(): left = lambda x: lax.ppermute(x, 'hits', bwd)  9.88 us
    unnamed x24, local copies, waits for them, and re-layouts  8.95 us
    pallas_call x5, Pallas kernels, attend(): local_call(functools.partial(attn_kernel, heads, blocks, rows), [jax.Shap...  8.58 us
    pallas_call x4, Pallas kernels, merge(): local_call(functools.partial(merge_kernel, heads, jobs, rows), outs, [vme...  7.11 us
  transfers between devices with their start and end apart: 30, of which 19 were waited for; matrix products, arithmetic and copies ran while one was open for 0% of the time, Pallas kernels for 27%

profile of v2, /device:TPU:0, one launch (start us, length us, event | category | flops | bytes accessed | tf_op | source)
XLA Modules:
  0.0 129.8 jit_solution(9536674210548388310)
XLA Ops:
  0.7 1.6 %copy-done = bf16[1024,1024]{1,0:T(8,128)(2,1)S(1)} copy-done((bf16[1024,1024]{1,0:T(8,128)(2,1)S(1)}, bf16[1024,1024]{1,0:T(8,128)(2,1)}, u32[]{:S(2)}) %copy-start) | copy-done | bytes 2097176
  2.2 1.2 copy-done.2
  3.5 1.2 copy-done.4
  6.5 3.1 %collective-permute-start = (bf16[528,128]{1,0:T(8,128)(2,1)}, bf16[528,128]{1,0:T(8,128)(2,1)S(1)}, u32[]{:S(2)}, u32[]{:S(2)}) collective-permute-start(bf16[528,128]{1,0:T(8,128)(2,1)} %get-tuple-element.45), channel_id=1, source_target_pairs={{0,4},{4,8},{8,12},{12,14},{14,10},{10,6},{6,2},{2,0},{1,5},{5,9},... | collective-permute-start | bytes 405512 | tf_op jit(solution)/shard_map/ppermute | solution.py:273
  9.6 1.2 copy-done.5
  10.8 2.1 %attend.8 = (f32[2048,128]{1,0:T(8,128)S(1)}, f32[16,256]{1,0:T(8,128)S(1)}) custom-call(s32[2]{0:T(128)S(1)} %pad_add_fusion.2.idx_ref, s32[1]{0:T(128)S(6)} %copy.10.cnt_ref, bf16[1024,1024]{1,0:T(8,128)(2,1)S(1)} %copy-done.1, bf16[512,1024]{1,0:T(8,128)(2,1)S(1)} %copy-done.3, bf16[512,1024]{1,0:T(8,128)(2,1)S(1)} %copy-done.5), custom_call_target="tpu_custom_call" | custom-call | flops 536870912 | bytes 1572864 | tf_op jit(solution)/shard_map/attend/pallas_call | solution.py:95
  13.3 1.3 %collective-permute-done.1.refs_3_ = bf16[528,128]{1,0:T(8,128)(2,1)S(1)} collective-permute-done((bf16[528,128]{1,0:T(8,128)(2,1)S(1)}, bf16[528,128]{1,0:T(8,128)(2,1)S(1)}, u32[]{:S(2)}, u32[]{:S(2)}) %collective-permute-start.1) | collective-permute-done | bytes 135200 | tf_op jit(solution)/shard_map/ppermute | solution.py:274
  14.6 1.3 merge.5
  15.8 1.6 %collective-permute-start.2 = (bf16[1056,128]{1,0:T(8,128)(2,1)}, bf16[1056,128]{1,0:T(8,128)(2,1)S(1)}, u32[]{:S(2)}, u32[]{:S(2)}) collective-permute-start(bf16[1056,128]{1,0:T(8,128)(2,1)} %get-tuple-element.47), channel_id=1, source_target_pairs={{0,4},{4,8},{8,12},{12,14},{14,10},{10,6},{6,2},{2,0},{1,5},{5,9},... | collective-permute-start | bytes 811016 | tf_op jit(solution)/shard_map/ppermute | solution.py:273
  18.4 1.2 copy-done.6
  19.7 2.1 %attend.7 = (f32[2048,128]{1,0:T(8,128)S(1)}, f32[16,256]{1,0:T(8,128)S(1)}) custom-call(s32[2]{0:T(128)S(1)} %pad_add_fusion.1.idx_ref, s32[1]{0:T(128)S(6)} %copy.10.cnt_ref, bf16[1024,1024]{1,0:T(8,128)(2,1)S(1)} %copy-done.1, bf16[512,1024]{1,0:T(8,128)(2,1)S(1)} %copy-done.3, bf16[512,1024]{1,0:T(8,128)(2,1)S(1)} %copy-done.6), custom_call_target="tpu_custom_call" | custom-call | flops 536870912 | bytes 1572864 | tf_op jit(solution)/shard_map/attend/pallas_call | solution.py:95
  21.8 1.3 %collective-permute-done.2.refs_2_ = bf16[1056,128]{1,0:T(8,128)(2,1)S(1)} collective-permute-done((bf16[1056,128]{1,0:T(8,128)(2,1)}, bf16[1056,128]{1,0:T(8,128)(2,1)S(1)}, u32[]{:S(2)}, u32[]{:S(2)}) %collective-permute-start.2) | collective-permute-done | bytes 270368 | tf_op jit(solution)/shard_map/ppermute | solution.py:273
  23.1 1.4 %collective-permute-done.3.refs_3_ = bf16[1056,128]{1,0:T(8,128)(2,1)} collective-permute-done((bf16[1056,128]{1,0:T(8,128)(2,1)}, bf16[1056,128]{1,0:T(8,128)(2,1)}, u32[]{:S(2)}, u32[]{:S(2)}) %collective-permute-start.3) | collective-permute-done | bytes 270368 | tf_op jit(solution)/shard_map/ppermute | solution.py:274
  24.5 2.6 %merge.6 = (bf16[1056,128]{1,0:T(8,128)(2,1)}, bf16[1056,128]{1,0:T(8,128)(2,1)}) custom-call(f32[2048,128]{1,0:T(8,128)S(1)} %get-tuple-element.39.refs_0_, f32[16,256]{1,0:T(8,128)S(1)} %get-tuple-element.40.refs_1_, bf16[1056,128]{1,0:T(8,128)(2,1)S(1)} %collective-permute-done.2.refs_2_, bf16[1056,128]{1,0:T(8,128)(2,1)} %collective-permute-done.3.refs_3_), custom_call_target="tpu_custom_call" | custom-call | flops 2162688 | bytes 2162688 | tf_op jit(solution)/shard_map/merge/pallas_call | solution.py:165
  27.1 1.6 %collective-permute-start.4 = (bf16[1056,128]{1,0:T(8,128)(2,1)}, bf16[1056,128]{1,0:T(8,128)(2,1)S(1)}, u32[]{:S(2)}, u32[]{:S(2)}) collective-permute-start(bf16[1056,128]{1,0:T(8,128)(2,1)} %get-tuple-element.49), channel_id=1, source_target_pairs={{0,4},{4,8},{8,12},{12,14},{14,10},{10,6},{6,2},{2,0},{1,5},{5,9},... | collective-permute-start | bytes 811016 | tf_op jit(solution)/shard_map/ppermute | solution.py:273
  29.2 1.2 copy-done.7
  30.4 2.1 %attend.6 = (f32[2048,128]{1,0:T(8,128)S(1)}, f32[16,256]{1,0:T(8,128)S(1)}) custom-call(s32[2]{0:T(128)S(1)} %pad_add_fusion.idx_ref, s32[1]{0:T(128)S(6)} %copy.10.cnt_ref, bf16[1024,1024]{1,0:T(8,128)(2,1)S(1)} %copy-done.1, bf16[512,1024]{1,0:T(8,128)(2,1)S(1)} %copy-done.3, bf16[512,1024]{1,0:T(8,128)(2,1)S(1)} %copy-done.7), custom_call_target="tpu_custom_call" | custom-call | flops 536870912 | bytes 1572864 | tf_op jit(solution)/shard_map/attend/pallas_call | solution.py:95
  32.6 1.2 collective-permute-done.4.refs_2_
  33.8 1.7 %collective-permute-done.5.refs_3_ = bf16[1056,128]{1,0:T(8,128)(2,1)} collective-permute-done((bf16[1056,128]{1,0:T(8,128)(2,1)}, bf16[1056,128]{1,0:T(8,128)(2,1)}, u32[]{:S(2)}, u32[]{:S(2)}) %collective-permute-start.5) | collective-permute-done | bytes 270368 | tf_op jit(solution)/shard_map/ppermute | solution.py:274
  35.5 2.6 %merge.7 = (bf16[1056,128]{1,0:T(8,128)(2,1)}, bf16[1056,128]{1,0:T(8,128)(2,1)}) custom-call(f32[2048,128]{1,0:T(8,128)S(1)} %get-tuple-element.37.refs_0_, f32[16,256]{1,0:T(8,128)S(1)} %get-tuple-element.38.refs_1_, bf16[1056,128]{1,0:T(8,128)(2,1)S(1)} %collective-permute-done.4.refs_2_, bf16[1056,128]{1,0:T(8,128)(2,1)} %collective-permute-done.5.refs_3_), custom_call_target="tpu_custom_call" | custom-call | flops 2162688 | bytes 2162688 | tf_op jit(solution)/shard_map/merge/pallas_call | solution.py:165
  38.0 1.5 %collective-permute-start.6 = (bf16[1056,128]{1,0:T(8,128)(2,1)}, bf16[1056,128]{1,0:T(8,128)(2,1)S(1)}, u32[]{:S(2)}, u32[]{:S(2)}) collective-permute-start(bf16[1056,128]{1,0:T(8,128)(2,1)} %get-tuple-element.51), channel_id=1, source_target_pairs={{0,4},{4,8},{8,12},{12,14},{14,10},{10,6},{6,2},{2,0},{1,5},{5,9},... | collective-permute-start | bytes 811016 | tf_op jit(solution)/shard_map/ppermute | solution.py:273
  40.1 1.2 copy-done.8
  41.3 1.1 attend.5
  42.4 2.3 %collective-permute-done.6.a_ref = bf16[1056,128]{1,0:T(8,128)(2,1)S(1)} collective-permute-done((bf16[1056,128]{1,0:T(8,128)(2,1)}, bf16[1056,128]{1,0:T(8,128)(2,1)S(1)}, u32[]{:S(2)}, u32[]{:S(2)}) %collective-permute-start.6) | collective-permute-done | bytes 270368 | tf_op jit(solution)/shard_map/ppermute | solution.py:273
  44.7 1.6 %collective-permute-done.7.b_ref = bf16[1056,128]{1,0:T(8,128)(2,1)} collective-permute-done((bf16[1056,128]{1,0:T(8,128)(2,1)}, bf16[1056,128]{1,0:T(8,128)(2,1)}, u32[]{:S(2)}, u32[]{:S(2)}) %collective-permute-start.7) | collective-permute-done | bytes 270368 | tf_op jit(solution)/shard_map/ppermute | solution.py:274
  46.3 2.4 %project.1 = (f32[64,2048]{1,0:T(8,128)S(1)}, f32[64,2048]{1,0:T(8,128)S(1)}) custom-call(s32[1]{0:T(128)} %bitcast.core_ref, f32[1024,128]{1,0:T(8,128)S(1)} %get-tuple-element.35.ctx_ref, f32[16,128]{1,0:T(8,128)S(1)} %get-tuple-element.36.st_ref, bf16[1056,128]{1,0:T(8,128)(2,1)S(1)} %collective-permute-done.6.a_ref, ...), custom_call_target="tpu_custom_call" | custom-call | flops 536870912 | bytes 5505024 | tf_op jit(solution)/shard_map/project/pallas_call | solution.py:212
  49.5 1.4 %collective-permute-done.10.gb_ref = f32[1,1024]{1,0:T(1,128)S(1)} collective-permute-done((f32[1,1024]{1,0:T(1,128)S(1)}, f32[1,1024]{1,0:T(1,128)S(1)}, u32[]{:S(2)}, u32[]{:S(2)}) %collective-permute-start.10) | collective-permute-done | bytes 4128 | tf_op jit(solution)/shard_map/ppermute | solution.py:275
  51.1 1.1 collective-permute-start.13
  53.2 6.3 %collective-permute-done.13.refs_0_ = bf16[64,2048]{1,0:T(8,128)(2,1)S(1)} collective-permute-done((bf16[64,2048]{1,0:T(8,128)(2,1)S(1)}, bf16[64,2048]{1,0:T(8,128)(2,1)S(1)}, u32[]{:S(2)}, u32[]{:S(2)}) %collective-permute-start.13) | collective-permute-done | bytes 262176 | tf_op jit(solution)/shard_map/ppermute | solution.py:273
  61.6 5.5 %collective-permute-done.15.refs_0_ = bf16[64,2048]{1,0:T(8,128)(2,1)S(1)} collective-permute-done((bf16[64,2048]{1,0:T(8,128)(2,1)S(1)}, bf16[64,2048]{1,0:T(8,128)(2,1)S(1)}, u32[]{:S(2)}, u32[]{:S(2)}) %collective-permute-start.15) | collective-permute-done | bytes 262176 | tf_op jit(solution)/shard_map/ppermute | solution.py:273
  69.1 4.6 %collective-permute-done.17.refs_0_ = bf16[64,2048]{1,0:T(8,128)(2,1)S(1)} collective-permute-done((bf16[64,2048]{1,0:T(8,128)(2,1)S(1)}, bf16[64,2048]{1,0:T(8,128)(2,1)S(1)}, u32[]{:S(2)}, u32[]{:S(2)}) %collective-permute-start.17) | collective-permute-done | bytes 262176 | tf_op jit(solution)/shard_map/ppermute | solution.py:273
  73.7 1.1 collective-permute-start.19
  74.8 1.2 collective-permute-start.20
  76.0 4.9 %ffn.7 = (f32[64,2048]{1,0:T(8,128)S(1)}, f32[64,2048]{1,0:T(8,128)S(1)}) custom-call(bf16[64,2048]{1,0:T(8,128)(2,1)S(1)} %collective-permute-done.15.refs_0_, bf16[64,2048]{1,0:T(8,128)(2,1)S(1)} %collective-permute-done.16.refs_1_, bf16[1024,1024]{1,0:T(8,128)(2,1)} %refs_2_.7, bf16[1024,1024]{1,0:T(8,128)(2,1)} %collective-permute-done.11.refs_2_.refs_3_, ...), custom_call_target="tpu_custom_call" | custom-call | flops 1073741824 | bytes 8388608 | tf_op jit(solution)/shard_map/ffn/pallas_call | solution.py:255
  80.9 5.1 %ffn.9 = (bf16[32,2048]{1,0:T(8,128)(2,1)S(1)}, bf16[32,2048]{1,0:T(8,128)(2,1)S(1)}) custom-call(bf16[32,2048]{1,0:T(8,128)(2,1)S(1)} %collective-permute-done.19.refs_0_, bf16[32,2048]{1,0:T(8,128)(2,1)S(1)} %collective-permute-done.20.refs_1_, bf16[1024,1024]{1,0:T(8,128)(2,1)} %refs_2_.7, bf16[1024,1024]{1,0:T(8,128)(2,1)} %collective-permute-done.11.refs_2_.refs_3_, ...), custom_call_target="tpu_custom_call" | custom-call | flops 536870912 | bytes 8388608 | tf_op jit(solution)/shard_map/ffn/pallas_call | solution.py:255
  86.0 1.1 collective-permute-start.21
  87.1 4.8 %ffn.6 = (f32[64,2048]{1,0:T(8,128)S(1)}, f32[64,2048]{1,0:T(8,128)S(1)}) custom-call(bf16[64,2048]{1,0:T(8,128)(2,1)S(1)} %collective-permute-done.13.refs_0_, bf16[64,2048]{1,0:T(8,128)(2,1)S(1)} %collective-permute-done.14.refs_1_, bf16[1024,1024]{1,0:T(8,128)(2,1)} %refs_2_.7, bf16[1024,1024]{1,0:T(8,128)(2,1)} %collective-permute-done.11.refs_2_.refs_3_, ...), custom_call_target="tpu_custom_call" | custom-call | flops 1073741824 | bytes 8388608 | tf_op jit(solution)/shard_map/ffn/pallas_call | solution.py:255
  91.9 4.9 %ffn.8 = (f32[64,2048]{1,0:T(8,128)S(1)}, f32[64,2048]{1,0:T(8,128)S(1)}) custom-call(bf16[64,2048]{1,0:T(8,128)(2,1)S(1)} %collective-permute-done.17.refs_0_, bf16[64,2048]{1,0:T(8,128)(2,1)S(1)} %collective-permute-done.18.refs_1_, bf16[1024,1024]{1,0:T(8,128)(2,1)} %refs_2_.7, bf16[1024,1024]{1,0:T(8,128)(2,1)} %collective-permute-done.11.refs_2_.refs_3_, ...), custom_call_target="tpu_custom_call" | custom-call | flops 1073741824 | bytes 8388608 | tf_op jit(solution)/shard_map/ffn/pallas_call | solution.py:255
  97.9 1.1 collective-permute-start.22
  99.0 4.2 %collective-permute-done.25 = bf16[32,2048]{1,0:T(8,128)(2,1)S(1)} collective-permute-done((bf16[32,2048]{1,0:T(8,128)(2,1)S(1)}, bf16[32,2048]{1,0:T(8,128)(2,1)S(1)}, u32[]{:S(2)}, u32[]{:S(2)}) %collective-permute-start.25) | collective-permute-done | bytes 131104 | tf_op jit(solution)/shard_map/ppermute | solution.py:274
  104.4 2.0 %collective-permute-done.22 = bf16[64,2048]{1,0:T(8,128)(2,1)S(1)} collective-permute-done((bf16[64,2048]{1,0:T(8,128)(2,1)S(1)}, bf16[64,2048]{1,0:T(8,128)(2,1)S(1)}, u32[]{:S(2)}, u32[]{:S(2)}) %collective-permute-start.22) | collective-permute-done | bytes 262176 | tf_op jit(solution)/shard_map/ppermute | solution.py:273
  106.4 1.1 collective-permute-start.23
  107.5 4.8 %collective-permute-done.26 = bf16[64,2048]{1,0:T(8,128)(2,1)S(1)} collective-permute-done((bf16[64,2048]{1,0:T(8,128)(2,1)S(1)}, bf16[64,2048]{1,0:T(8,128)(2,1)S(1)}, u32[]{:S(2)}, u32[]{:S(2)}) %collective-permute-start.26) | collective-permute-done | bytes 262176 | tf_op jit(solution)/shard_map/ppermute | solution.py:274
  113.4 2.2 %collective-permute-done.23 = bf16[64,2048]{1,0:T(8,128)(2,1)S(1)} collective-permute-done((bf16[64,2048]{1,0:T(8,128)(2,1)S(1)}, bf16[64,2048]{1,0:T(8,128)(2,1)S(1)}, u32[]{:S(2)}, u32[]{:S(2)}) %collective-permute-start.23) | collective-permute-done | bytes 262176 | tf_op jit(solution)/shard_map/ppermute | solution.py:273
  115.7 1.1 collective-permute-start.24
  116.7 4.2 %collective-permute-done.27 = bf16[64,2048]{1,0:T(8,128)(2,1)S(1)} collective-permute-done((bf16[64,2048]{1,0:T(8,128)(2,1)S(1)}, bf16[64,2048]{1,0:T(8,128)(2,1)S(1)}, u32[]{:S(2)}, u32[]{:S(2)}) %collective-permute-start.27) | collective-permute-done | bytes 262176 | tf_op jit(solution)/shard_map/ppermute | solution.py:274
  122.1 5.1 %ffn.5 = f32[64,2048]{1,0:T(8,128)S(1)} custom-call(bf16[64,2048]{1,0:T(8,128)(2,1)S(1)} %get-tuple-element.56.refs_0_, bf16[1024,1024]{1,0:T(8,128)(2,1)} %refs_2_.7, bf16[1024,1024]{1,0:T(8,128)(2,1)} %collective-permute-done.11.refs_2_.refs_3_, bf16[1024,1024]{1,0:T(8,128)(2,1)} %refs_4_.7, bf16[1024,1024]{1,0:T(8,128)(2,1)} %collective-permute-done.12.refs_4_.refs_5_), custom_call_target="tpu_custom_call" | custom-call | flops 536870912 | bytes 8388608 | tf_op jit(solution)/shard_map/ffn/pallas_call | solution.py:255
  127.7 1.3 %collective-permute-done.29 = bf16[64,1024]{1,0:T(8,128)(2,1)S(1)} collective-permute-done((bf16[64,1024]{1,0:T(8,128)(2,1)S(1)}, bf16[64,1024]{1,0:T(8,128)(2,1)S(1)}, u32[]{:S(2)}, u32[]{:S(2)}) %collective-permute-start.29) | collective-permute-done | bytes 131104 | tf_op jit(solution)/shard_map/ppermute | solution.py:275
  (71 shorter events, 16.0 us)
Async XLA Ops:
  0.7 1.6 %copy-start = (bf16[1024,1024]{1,0:T(8,128)(2,1)S(1)}, bf16[1024,1024]{1,0:T(8,128)(2,1)}, u32[]{:S(2)}) copy-start(bf16[1024,1024]{1,0:T(8,128)(2,1)} %q_ref.9) | copy-start | bytes 6291460
  2.2 1.2 copy-start.2
  3.5 1.2 copy-start.4
  4.7 4.9 %copy-start.1 = (bf16[1024,1024]{1,0:T(8,128)(2,1)S(1)}, bf16[1024,1024]{1,0:T(8,128)(2,1)}, u32[]{:S(2)}) copy-start(bf16[1024,1024]{1,0:T(8,128)(2,1)} %q_ref.9) | copy-start | bytes 6291460
  4.7 4.9 %copy-start.3 = (bf16[512,1024]{1,0:T(8,128)(2,1)S(1)}, bf16[512,1024]{1,0:T(8,128)(2,1)}, u32[]{:S(2)}) copy-start(bf16[512,1024]{1,0:T(8,128)(2,1)} %k_ref.9) | copy-start | bytes 3145732
  6.5 6.8 %collective-permute-start = (bf16[528,128]{1,0:T(8,128)(2,1)}, bf16[528,128]{1,0:T(8,128)(2,1)S(1)}, u32[]{:S(2)}, u32[]{:S(2)}) collective-permute-start(bf16[528,128]{1,0:T(8,128)(2,1)} %get-tuple-element.45), channel_id=1, source_target_pairs={{0,4},{4,8},{8,12},{12,14},{14,10},{10,6},{6,2},{2,0},{1,5},{5,9},... | collective-permute-start | bytes 405512 | tf_op jit(solution)/shard_map/ppermute | solution.py:273
  9.5 5.0 %collective-permute-start.1 = (bf16[528,128]{1,0:T(8,128)(2,1)S(1)}, bf16[528,128]{1,0:T(8,128)(2,1)S(1)}, u32[]{:S(2)}, u32[]{:S(2)}) collective-permute-start(bf16[528,128]{1,0:T(8,128)(2,1)S(1)} %get-tuple-element.46), channel_id=1, source_target_pairs={{4,0},{8,4},{12,8},{14,12},{10,14},{6,10},{2,6},{0,2},{5,1},{9,5},... | collective-permute-start | bytes 405512 | tf_op jit(solution)/shard_map/ppermute | solution.py:274
  9.6 1.2 copy-start.5
  15.8 7.3 %collective-permute-start.2 = (bf16[1056,128]{1,0:T(8,128)(2,1)}, bf16[1056,128]{1,0:T(8,128)(2,1)S(1)}, u32[]{:S(2)}, u32[]{:S(2)}) collective-permute-start(bf16[1056,128]{1,0:T(8,128)(2,1)} %get-tuple-element.47), channel_id=1, source_target_pairs={{0,4},{4,8},{8,12},{12,14},{14,10},{10,6},{6,2},{2,0},{1,5},{5,9},... | collective-permute-start | bytes 811016 | tf_op jit(solution)/shard_map/ppermute | solution.py:273
  17.4 7.1 %collective-permute-start.3 = (bf16[1056,128]{1,0:T(8,128)(2,1)}, bf16[1056,128]{1,0:T(8,128)(2,1)}, u32[]{:S(2)}, u32[]{:S(2)}) collective-permute-start(bf16[1056,128]{1,0:T(8,128)(2,1)} %get-tuple-element.48), channel_id=1, source_target_pairs={{4,0},{8,4},{12,8},{14,12},{10,14},{6,10},{2,6},{0,2},{5,1},{9,5},... | collective-permute-start | bytes 811016 | tf_op jit(solution)/shard_map/ppermute | solution.py:274
  17.9 58.2 %collective-permute-start.11 = (bf16[1024,1024]{1,0:T(8,128)(2,1)}, bf16[1024,1024]{1,0:T(8,128)(2,1)}, u32[]{:S(2)}, u32[]{:S(2)}) collective-permute-start(bf16[1024,1024]{1,0:T(8,128)(2,1)} %refs_2_.7), channel_id=1, source_target_pairs={{0,1},{1,0},{2,3},{3,2},{4,5},{5,4},{6,7},{7,6},{8,9},{9,8},{10,11... | collective-permute-start | bytes 6291464 | tf_op jit(solution)/shard_map/ppermute | solution.py:275
  17.9 58.2 %collective-permute-start.12 = (bf16[1024,1024]{1,0:T(8,128)(2,1)}, bf16[1024,1024]{1,0:T(8,128)(2,1)}, u32[]{:S(2)}, u32[]{:S(2)}) collective-permute-start(bf16[1024,1024]{1,0:T(8,128)(2,1)} %refs_4_.7), channel_id=1, source_target_pairs={{0,1},{1,0},{2,3},{3,2},{4,5},{5,4},{6,7},{7,6},{8,9},{9,8},{10,11... | collective-permute-start | bytes 6291464 | tf_op jit(solution)/shard_map/ppermute | solution.py:275
  18.4 1.2 copy-start.6
  27.1 6.7 %collective-permute-start.4 = (bf16[1056,128]{1,0:T(8,128)(2,1)}, bf16[1056,128]{1,0:T(8,128)(2,1)S(1)}, u32[]{:S(2)}, u32[]{:S(2)}) collective-permute-start(bf16[1056,128]{1,0:T(8,128)(2,1)} %get-tuple-element.49), channel_id=1, source_target_pairs={{0,4},{4,8},{8,12},{12,14},{14,10},{10,6},{6,2},{2,0},{1,5},{5,9},... | collective-permute-start | bytes 811016 | tf_op jit(solution)/shard_map/ppermute | solution.py:273
  28.7 6.8 %collective-permute-start.5 = (bf16[1056,128]{1,0:T(8,128)(2,1)}, bf16[1056,128]{1,0:T(8,128)(2,1)}, u32[]{:S(2)}, u32[]{:S(2)}) collective-permute-start(bf16[1056,128]{1,0:T(8,128)(2,1)} %get-tuple-element.50), channel_id=1, source_target_pairs={{4,0},{8,4},{12,8},{14,12},{10,14},{6,10},{2,6},{0,2},{5,1},{9,5},... | collective-permute-start | bytes 811016 | tf_op jit(solution)/shard_map/ppermute | solution.py:274
  29.2 1.2 copy-start.7
  38.0 6.7 %collective-permute-start.6 = (bf16[1056,128]{1,0:T(8,128)(2,1)}, bf16[1056,128]{1,0:T(8,128)(2,1)S(1)}, u32[]{:S(2)}, u32[]{:S(2)}) collective-permute-start(bf16[1056,128]{1,0:T(8,128)(2,1)} %get-tuple-element.51), channel_id=1, source_target_pairs={{0,4},{4,8},{8,12},{12,14},{14,10},{10,6},{6,2},{2,0},{1,5},{5,9},... | collective-permute-start | bytes 811016 | tf_op jit(solution)/shard_map/ppermute | solution.py:273
  39.6 6.8 %collective-permute-start.7 = (bf16[1056,128]{1,0:T(8,128)(2,1)}, bf16[1056,128]{1,0:T(8,128)(2,1)}, u32[]{:S(2)}, u32[]{:S(2)}) collective-permute-start(bf16[1056,128]{1,0:T(8,128)(2,1)} %get-tuple-element.52), channel_id=1, source_target_pairs={{4,0},{8,4},{12,8},{14,12},{10,14},{6,10},{2,6},{0,2},{5,1},{9,5},... | collective-permute-start | bytes 811016 | tf_op jit(solution)/shard_map/ppermute | solution.py:274
  40.1 1.2 copy-start.8
  41.3 5.1 %copy-start.9 = (bf16[1024,2048]{1,0:T(8,128)(2,1)S(1)}, bf16[1024,2048]{1,0:T(8,128)(2,1)}, u32[]{:S(2)}) copy-start(bf16[1024,2048]{1,0:T(8,128)(2,1)} %w_ref.1) | copy-start | bytes 12582916
  46.3 2.5 %copy-start.11 = (bf16[128,1024]{1,0:T(8,128)(2,1)S(1)}, bf16[128,1024]{1,0:T(8,128)(2,1)}, u32[]{:S(2)}) copy-start(bf16[128,1024]{1,0:T(8,128)(2,1)} %param.13) | copy-start | bytes 786436
  46.3 3.1 %copy-start.10 = (f32[1024]{0:T(1024)S(1)}, f32[1024]{0:T(1024)}, u32[]{:S(2)}) copy-start(f32[1024]{0:T(1024)} %param.15) | copy-start | bytes 12292
  48.8 2.2 %collective-permute-start.8 = (f32[64,2048]{1,0:T(8,128)S(1)}, f32[64,2048]{1,0:T(8,128)S(1)}, u32[]{:S(2)}, u32[]{:S(2)}) collective-permute-start(f32[64,2048]{1,0:T(8,128)S(1)} %get-tuple-element.54), channel_id=1, source_target_pairs={{0,1},{1,0},{2,3},{3,2},{4,5},{5,4},{6,7},{7,6},{8,9},{9,8},{10,11... | collective-permute-start | bytes 1572872 | tf_op jit(solution)/shard_map/ppermute | solution.py:275
  48.9 2.0 %collective-permute-start.9 = (bf16[64,1024]{1,0:T(8,128)(2,1)S(1)}, bf16[64,1024]{1,0:T(8,128)(2,1)S(1)}, u32[]{:S(2)}, u32[]{:S(2)}) collective-permute-start(bf16[64,1024]{1,0:T(8,128)(2,1)S(1)} %get-tuple-element.67), channel_id=1, source_target_pairs={{0,1},{1,0},{2,3},{3,2},{4,5},{5,4},{6,7},{7,6},{8,9},{9,8},{10,11... | collective-permute-start | bytes 393224 | tf_op jit(solution)/shard_map/ppermute | solution.py:275
  49.4 1.5 %collective-permute-start.10 = (f32[1,1024]{1,0:T(1,128)S(1)}, f32[1,1024]{1,0:T(1,128)S(1)}, u32[]{:S(2)}, u32[]{:S(2)}) collective-permute-start(f32[1,1024]{1,0:T(1,128)S(1)} %bitcast.10), channel_id=1, source_target_pairs={{0,1},{1,0},{2,3},{3,2},{4,5},{5,4},{6,7},{7,6},{8,9},{9,8},{10,11... | collective-permute-start | bytes 12296 | tf_op jit(solution)/shard_map/ppermute | solution.py:275
  51.1 8.4 %collective-permute-start.13 = (bf16[64,2048]{1,0:T(8,128)(2,1)S(1)}, bf16[64,2048]{1,0:T(8,128)(2,1)S(1)}, u32[]{:S(2)}, u32[]{:S(2)}) collective-permute-start(bf16[64,2048]{1,0:T(8,128)(2,1)S(1)} %get-tuple-element.56.refs_0_), channel_id=1, source_target_pairs={{0,4},{4,8},{8,12},{12,14},{14,10},{10,6},{6,2},{2,0},{1,5},{5,9},... | collective-permute-start | bytes 786440 | tf_op jit(solution)/shard_map/ppermute | solution.py:273
  52.2 8.4 %collective-permute-start.14 = (bf16[64,2048]{1,0:T(8,128)(2,1)S(1)}, bf16[64,2048]{1,0:T(8,128)(2,1)S(1)}, u32[]{:S(2)}, u32[]{:S(2)}) collective-permute-start(bf16[64,2048]{1,0:T(8,128)(2,1)S(1)} %get-tuple-element.56.refs_0_), channel_id=1, source_target_pairs={{4,0},{8,4},{12,8},{14,12},{10,14},{6,10},{2,6},{0,2},{5,1},{9,5},... | collective-permute-start | bytes 786440 | tf_op jit(solution)/shard_map/ppermute | solution.py:274
  59.5 7.5 %collective-permute-start.15 = (bf16[64,2048]{1,0:T(8,128)(2,1)S(1)}, bf16[64,2048]{1,0:T(8,128)(2,1)S(1)}, u32[]{:S(2)}, u32[]{:S(2)}) collective-permute-start(bf16[64,2048]{1,0:T(8,128)(2,1)S(1)} %collective-permute-done.13.refs_0_), channel_id=1, source_target_pairs={{0,4},{4,8},{8,12},{12,14},{14,10},{10,6},{6,2},{2,0},{1,5},{5,9},... | collective-permute-start | bytes 786440 | tf_op jit(solution)/shard_map/ppermute | solution.py:273
  60.6 7.5 %collective-permute-start.16 = (bf16[64,2048]{1,0:T(8,128)(2,1)S(1)}, bf16[64,2048]{1,0:T(8,128)(2,1)S(1)}, u32[]{:S(2)}, u32[]{:S(2)}) collective-permute-start(bf16[64,2048]{1,0:T(8,128)(2,1)S(1)} %collective-permute-done.14.refs_1_), channel_id=1, source_target_pairs={{4,0},{8,4},{12,8},{14,12},{10,14},{6,10},{2,6},{0,2},{5,1},{9,5},... | collective-permute-start | bytes 786440 | tf_op jit(solution)/shard_map/ppermute | solution.py:274
  67.0 6.6 %collective-permute-start.17 = (bf16[64,2048]{1,0:T(8,128)(2,1)S(1)}, bf16[64,2048]{1,0:T(8,128)(2,1)S(1)}, u32[]{:S(2)}, u32[]{:S(2)}) collective-permute-start(bf16[64,2048]{1,0:T(8,128)(2,1)S(1)} %collective-permute-done.15.refs_0_), channel_id=1, source_target_pairs={{0,4},{4,8},{8,12},{12,14},{14,10},{10,6},{6,2},{2,0},{1,5},{5,9},... | collective-permute-start | bytes 786440 | tf_op jit(solution)/shard_map/ppermute | solution.py:273
  68.1 6.7 %collective-permute-start.18 = (bf16[64,2048]{1,0:T(8,128)(2,1)S(1)}, bf16[64,2048]{1,0:T(8,128)(2,1)S(1)}, u32[]{:S(2)}, u32[]{:S(2)}) collective-permute-start(bf16[64,2048]{1,0:T(8,128)(2,1)S(1)} %collective-permute-done.16.refs_1_), channel_id=1, source_target_pairs={{4,0},{8,4},{12,8},{14,12},{10,14},{6,10},{2,6},{0,2},{5,1},{9,5},... | collective-permute-start | bytes 786440 | tf_op jit(solution)/shard_map/ppermute | solution.py:274
  73.7 7.2 %collective-permute-start.19 = (bf16[32,2048]{1,0:T(8,128)(2,1)S(1)}, bf16[32,2048]{1,0:T(8,128)(2,1)S(1)}, u32[]{:S(2)}, u32[]{:S(2)}) collective-permute-start(bf16[32,2048]{1,0:T(8,128)(2,1)S(1)} %slice.34), channel_id=1, source_target_pairs={{0,4},{4,8},{8,12},{12,14},{14,10},{10,6},{6,2},{2,0},{1,5},{5,9},... | collective-permute-start | bytes 393224 | tf_op jit(solution)/shard_map/ppermute | solution.py:273
  74.8 6.1 %collective-permute-start.20 = (bf16[32,2048]{1,0:T(8,128)(2,1)S(1)}, bf16[32,2048]{1,0:T(8,128)(2,1)S(1)}, u32[]{:S(2)}, u32[]{:S(2)}) collective-permute-start(bf16[32,2048]{1,0:T(8,128)(2,1)S(1)} %slice.35), channel_id=1, source_target_pairs={{4,0},{8,4},{12,8},{14,12},{10,14},{6,10},{2,6},{0,2},{5,1},{9,5},... | collective-permute-start | bytes 393224 | tf_op jit(solution)/shard_map/ppermute | solution.py:274
  86.0 11.9 %collective-permute-start.21 = (bf16[32,2048]{1,0:T(8,128)(2,1)S(1)}, bf16[32,2048]{1,0:T(8,128)(2,1)S(1)}, u32[]{:S(2)}, u32[]{:S(2)}) collective-permute-start(bf16[32,2048]{1,0:T(8,128)(2,1)S(1)} %get-tuple-element.60), channel_id=1, source_target_pairs={{0,4},{4,8},{8,12},{12,14},{14,10},{10,6},{6,2},{2,0},{1,5},{5,9},... | collective-permute-start | bytes 393224 | tf_op jit(solution)/shard_map/ppermute | solution.py:273
  96.8 6.4 %collective-permute-start.25 = (bf16[32,2048]{1,0:T(8,128)(2,1)S(1)}, bf16[32,2048]{1,0:T(8,128)(2,1)S(1)}, u32[]{:S(2)}, u32[]{:S(2)}) collective-permute-start(bf16[32,2048]{1,0:T(8,128)(2,1)S(1)} %get-tuple-element.64), channel_id=1, source_target_pairs={{4,0},{8,4},{12,8},{14,12},{10,14},{6,10},{2,6},{0,2},{5,1},{9,5},... | collective-permute-start | bytes 393224 | tf_op jit(solution)/shard_map/ppermute | solution.py:274
  97.9 8.4 %collective-permute-start.22 = (bf16[64,2048]{1,0:T(8,128)(2,1)S(1)}, bf16[64,2048]{1,0:T(8,128)(2,1)S(1)}, u32[]{:S(2)}, u32[]{:S(2)}) collective-permute-start(bf16[64,2048]{1,0:T(8,128)(2,1)S(1)} %pad_maximum_fusion), channel_id=1, source_target_pairs={{0,4},{4,8},{8,12},{12,14},{14,10},{10,6},{6,2},{2,0},{1,5},{5,9},... | collective-permute-start | bytes 786440 | tf_op jit(solution)/shard_map/ppermute | solution.py:273
  103.3 9.0 %collective-permute-start.26 = (bf16[64,2048]{1,0:T(8,128)(2,1)S(1)}, bf16[64,2048]{1,0:T(8,128)(2,1)S(1)}, u32[]{:S(2)}, u32[]{:S(2)}) collective-permute-start(bf16[64,2048]{1,0:T(8,128)(2,1)S(1)} %pad_maximum_fusion.1), channel_id=1, source_target_pairs={{4,0},{8,4},{12,8},{14,12},{10,14},{6,10},{2,6},{0,2},{5,1},{9,5},... | collective-permute-start | bytes 786440 | tf_op jit(solution)/shard_map/ppermute | solution.py:274
  106.4 9.2 %collective-permute-start.23 = (bf16[64,2048]{1,0:T(8,128)(2,1)S(1)}, bf16[64,2048]{1,0:T(8,128)(2,1)S(1)}, u32[]{:S(2)}, u32[]{:S(2)}) collective-permute-start(bf16[64,2048]{1,0:T(8,128)(2,1)S(1)} %add_convert_fusion.4), channel_id=1, source_target_pairs={{0,4},{4,8},{8,12},{12,14},{14,10},{10,6},{6,2},{2,0},{1,5},{5,9},... | collective-permute-start | bytes 786440 | tf_op jit(solution)/shard_map/ppermute | solution.py:273
  112.3 8.6 %collective-permute-start.27 = (bf16[64,2048]{1,0:T(8,128)(2,1)S(1)}, bf16[64,2048]{1,0:T(8,128)(2,1)S(1)}, u32[]{:S(2)}, u32[]{:S(2)}) collective-permute-start(bf16[64,2048]{1,0:T(8,128)(2,1)S(1)} %add_convert_fusion.2), channel_id=1, source_target_pairs={{4,0},{8,4},{12,8},{14,12},{10,14},{6,10},{2,6},{0,2},{5,1},{9,5},... | collective-permute-start | bytes 786440 | tf_op jit(solution)/shard_map/ppermute | solution.py:274
  115.7 11.5 %collective-permute-start.24 = (bf16[64,2048]{1,0:T(8,128)(2,1)S(1)}, bf16[64,2048]{1,0:T(8,128)(2,1)S(1)}, u32[]{:S(2)}, u32[]{:S(2)}) collective-permute-start(bf16[64,2048]{1,0:T(8,128)(2,1)S(1)} %add_convert_fusion.3), channel_id=1, source_target_pairs={{0,4},{4,8},{8,12},{12,14},{14,10},{10,6},{6,2},{2,0},{1,5},{5,9},... | collective-permute-start | bytes 786440 | tf_op jit(solution)/shard_map/ppermute | solution.py:273
  121.0 6.4 %collective-permute-start.28 = (bf16[64,2048]{1,0:T(8,128)(2,1)S(1)}, bf16[64,2048]{1,0:T(8,128)(2,1)S(1)}, u32[]{:S(2)}, u32[]{:S(2)}) collective-permute-start(bf16[64,2048]{1,0:T(8,128)(2,1)S(1)} %add_convert_fusion.1), channel_id=1, source_target_pairs={{4,0},{8,4},{12,8},{14,12},{10,14},{6,10},{2,6},{0,2},{5,1},{9,5},... | collective-permute-start | bytes 786440 | tf_op jit(solution)/shard_map/ppermute | solution.py:274
  127.6 1.4 %collective-permute-start.29 = (bf16[64,1024]{1,0:T(8,128)(2,1)S(1)}, bf16[64,1024]{1,0:T(8,128)(2,1)S(1)}, u32[]{:S(2)}, u32[]{:S(2)}) collective-permute-start(bf16[64,1024]{1,0:T(8,128)(2,1)S(1)} %get-tuple-element.66), channel_id=1, source_target_pairs={{0,1},{1,0},{2,3},{3,2},{4,5},{5,4},{6,7},{7,6},{8,9},{9,8},{10,11... | collective-permute-start | bytes 393224 | tf_op jit(solution)/shard_map/ppermute | solution.py:275
